TPU v7x, 256 devices: a whole 4x4x8 slice. The times are simulated.
256 devices in a mesh: seq: 64 (over z_hi, y, x, core), tp: 4 (over z_lo).
Axes of the slice: x: 4, y: 4, z: 8 (z_hi: 2, z_lo: 4; z = z_hi * 4 + z_lo), core: 2. Of those that a mesh axis runs over, the one named last changes fastest.
Arguments:
- tokens: bfloat16 [8192, 2048], P(('seq', 'tp')), may hold values from -6 to 6
- block_ids: int32 [64, 2], replicated, may hold values from 0 to 127, as said below
- attn_gain: float32 [2048], replicated, may hold values from 0.25 to 1.75
- q_weight: bfloat16 [2048, 3072], P(None, 'tp'), may hold values from -0.125 to 0.125
- kv_weight: bfloat16 [2048, 576], replicated, may hold values from -0.125 to 0.125
- kv_gain: float32 [512], replicated, may hold values from 0.25 to 1.75
- uk_weight: bfloat16 [16, 512, 128], P('tp'), may hold values from -40 to 40
- uv_weight: bfloat16 [16, 512, 128], P('tp'), may hold values from -0.25 to 0.25
- o_weight: bfloat16 [2048, 2048], P('tp'), may hold values from -0.125 to 0.125
- ffn_gain: float32 [2048], replicated, may hold values from 0.25 to 1.75
- w_gate: bfloat16 [64, 2048, 1408], P('seq', None, 'tp'), may hold values from -0.125 to 0.125
- w_up: bfloat16 [64, 2048, 1408], P('seq', None, 'tp'), may hold values from -0.125 to 0.125
- w_down: bfloat16 [64, 1408, 2048], P('seq', 'tp'), may hold values from -0.15625 to 0.15625
- routes: int32 [8192, 6], P('seq'), may hold values from 0 to 63, all different within a row; in each aligned block of 32 rows (0 to 31, 32 to 63, ...) at most 4 rows name the same one
- gate_weights: float32 [8192, 6], P('seq'), may hold values from 0.1 to 1
Outputs:
- layer_out: bfloat16 [8192, 2048], P(('seq', 'tp'))
Inputs may be any that keep to these rules, and one draw needn't show every extreme that they name: `block_ids`: row d is (b, 127 - b) with b below 64; the first column names every b once. `routes`: each row names 6 different experts. In each aligned block of 32 rows (the tokens of one device) no expert is named by more than 4 rows, a bound that some block reaches.
All inputs are finite; a program needn't handle non-finite values.
Results may differ from a plain program's by a relative error of at most 0.027.
The roundings to bfloat16 on the way count: a program that leaves them out, or rounds other values in their place, can miss the bound.
Values may be sent and summed in bfloat16 or wider, within the bound.
A program may use at most 128 MiB of HBM per device.

v0:
```python
import math

import jax
import jax.numpy as jnp
from jax import lax
from jax.sharding import PartitionSpec as P

EPSILON = 1e-06


def normalize(values, gain_vec):
    values = values.astype(jnp.float32)
    factor = lax.rsqrt(jnp.mean(values * values, axis=-1, keepdims=True) + EPSILON)
    return values * factor * gain_vec


def rotate(values, position):
    half_width = values.shape[-1] // 2
    frequency = jnp.exp(
        jnp.arange(half_width, dtype=jnp.float32) * (-2.0 * math.log(10000.0) / values.shape[-1])
    )
    angles = (
        position.astype(jnp.float32).reshape(position.shape + (1,) * (values.ndim - 1)) * frequency
    )
    cosine = jnp.cos(angles)
    sine_part = jnp.sin(angles)
    first_half = values[..., :half_width]
    second_half = values[..., half_width:]
    return jnp.concatenate(
        [
            first_half * cosine - second_half * sine_part,
            second_half * cosine + first_half * sine_part,
        ],
        axis=-1,
    )


def positions(row_ids, block_ids, rows_dev):
    half_width = rows_dev // 2
    device = row_ids // rows_dev
    within = row_ids % rows_dev
    block_num = block_ids.reshape(-1)[device * 2 + within // half_width]
    return block_num * half_width + within % half_width


def body(
    tokens,
    block_ids,
    attn_gain,
    q_weight,
    kv_weight,
    kv_gain,
    uk_weight,
    uv_weight,
    o_weight,
    ffn_gain,
    w_gate,
    w_up,
    w_down,
    routes,
    gate_weights,
):
    tp_count = lax.axis_size("tp")
    seq_count = lax.axis_size("seq")
    tp_index = lax.axis_index("tp")
    seq_index = lax.axis_index("seq")
    sub_rows = tokens.shape[0]
    dev_rows = sub_rows * tp_count
    model_dim = tokens.shape[1]
    head_count = uk_weight.shape[0]
    latent_dim = uk_weight.shape[1]
    nope_dim = uk_weight.shape[2]
    rope_dim = kv_weight.shape[1] - latent_dim
    value_dim = uv_weight.shape[2]
    top_count = routes.shape[1]
    capacity = min(sub_rows, max(2, 3 * sub_rows * top_count // (2 * seq_count)))
    score_scale = (nope_dim + rope_dim) ** (-0.5)
    all_tokens = lax.all_gather(tokens, "tp", axis=0, tiled=True)
    normed = normalize(all_tokens, attn_gain).astype(jnp.bfloat16)
    query_ids = seq_index * dev_rows + jnp.arange(dev_rows, dtype=jnp.int32)
    query_pos = positions(query_ids, block_ids, dev_rows)
    queries = jnp.dot(normed, q_weight, preferred_element_type=jnp.float32).astype(jnp.bfloat16)
    queries = queries.reshape(dev_rows, head_count, nope_dim + rope_dim)
    query_rope = rotate(queries[..., nope_dim:].astype(jnp.float32), query_pos).astype(jnp.bfloat16)
    query_latent = jnp.einsum(
        "thn,hln->thl", queries[..., :nope_dim], uk_weight, preferred_element_type=jnp.float32
    ).astype(jnp.bfloat16)
    projected = jnp.dot(normed, kv_weight, preferred_element_type=jnp.float32)
    latent = normalize(projected[:, :latent_dim], kv_gain).astype(jnp.bfloat16)
    key_rope = rotate(projected[:, latent_dim:], query_pos).astype(jnp.bfloat16)
    latent, key_rope = (latent, key_rope)
    run_max = jnp.full((dev_rows, head_count), -1e30, jnp.float32)
    piece_latent = lax.all_gather(latent, "seq", axis=0, tiled=True)
    piece_rope = lax.all_gather(key_rope, "seq", axis=0, tiled=True)
    count_rows = piece_latent.shape[0]
    key_pos = positions(jnp.arange(count_rows, dtype=jnp.int32), block_ids, dev_rows)
    scores = jnp.einsum(
        "thl,kl->thk", query_latent, piece_latent, preferred_element_type=jnp.float32
    )
    scores = scores + jnp.einsum(
        "thr,kr->thk", query_rope, piece_rope, preferred_element_type=jnp.float32
    )
    scores = scores * score_scale
    allowed = key_pos[None, None, :] <= query_pos[:, None, None]
    scores = jnp.where(allowed, scores, -1e30)
    new_max = jnp.maximum(run_max, jnp.max(scores, axis=-1))
    exp_terms = jnp.where(allowed, jnp.exp(scores - new_max[..., None]), 0.0)
    run_sum = jnp.sum(exp_terms, axis=-1)
    accumulated = jnp.einsum(
        "thk,kl->thl",
        exp_terms.astype(jnp.bfloat16),
        piece_latent,
        preferred_element_type=jnp.float32,
    )
    folded = (new_max, run_sum, accumulated)
    run_max, run_sum, accumulated = folded
    out_latent = (accumulated / run_sum[..., None]).astype(jnp.bfloat16)
    head_out = jnp.einsum(
        "thl,hlv->thv", out_latent, uv_weight, preferred_element_type=jnp.float32
    ).astype(jnp.bfloat16)
    partial_out = jnp.dot(
        head_out.reshape(dev_rows, head_count * value_dim),
        o_weight,
        preferred_element_type=jnp.float32,
    )
    expert_ids = jnp.arange(seq_count, dtype=jnp.int32)

    def slot_table(route_rows):
        flat_ids = route_rows.reshape(-1)
        onehot = (flat_ids[:, None] == expert_ids[None, :]).astype(jnp.int32)
        rank_table = jnp.cumsum(onehot, axis=0) - onehot
        return flat_ids * capacity + jnp.sum(rank_table * onehot, axis=1)

    own_routes = lax.dynamic_slice_in_dim(routes, tp_index * sub_rows, sub_rows, 0)
    own_weights = lax.dynamic_slice_in_dim(gate_weights, tp_index * sub_rows, sub_rows, 0)
    attn_own = lax.psum_scatter(
        partial_out.astype(jnp.bfloat16), "tp", scatter_dimension=0, tiled=True
    ).astype(jnp.float32)
    mixed_rows = (tokens.astype(jnp.float32) + attn_own).astype(jnp.bfloat16)
    normed_own = normalize(mixed_rows, ffn_gain).astype(jnp.bfloat16)
    target = slot_table(own_routes)
    source = jnp.arange(target.shape[0], dtype=jnp.int32) // top_count
    buffer = (
        jnp.zeros((seq_count * capacity, model_dim), jnp.bfloat16)
        .at[target]
        .set(normed_own[source])
    )
    packed = buffer.reshape(seq_count, capacity, model_dim)
    arrived = lax.all_to_all(packed, "seq", split_axis=0, concat_axis=0, tiled=True)
    piece_data = lax.all_gather(arrived, "tp", axis=0, tiled=True)
    flat_rows = piece_data.reshape(-1, model_dim)
    gate_part = jnp.dot(flat_rows, w_gate[0], preferred_element_type=jnp.float32)
    up_part = jnp.dot(flat_rows, w_up[0], preferred_element_type=jnp.float32)
    hidden = (
        (jax.nn.silu(gate_part) * up_part)
        .astype(jnp.bfloat16)
        .reshape(piece_data.shape[0], capacity, -1)
        .reshape(-1, w_up.shape[2])
    )
    down_local = w_down[0]
    expert_out = lax.psum_scatter(
        jnp.dot(hidden, down_local, preferred_element_type=jnp.float32).astype(jnp.bfloat16),
        "tp",
        scatter_dimension=0,
        tiled=True,
    ).astype(jnp.float32)
    expert_out = expert_out.astype(jnp.bfloat16).reshape(seq_count, capacity, model_dim)
    returned = lax.all_to_all(expert_out, "seq", split_axis=0, concat_axis=0, tiled=True).reshape(
        seq_count * capacity, model_dim
    )
    picked = (
        returned[slot_table(own_routes)].astype(jnp.float32).reshape(sub_rows, top_count, model_dim)
    )
    combined = jnp.sum(picked * own_weights[..., None], axis=1)
    return (mixed_rows.astype(jnp.float32) + combined).astype(jnp.bfloat16)


def solution(mesh):
    return jax.shard_map(
        body,
        mesh=mesh,
        in_specs=(
            P(("seq", "tp"), None),
            P(),
            P(),
            P(None, "tp"),
            P(),
            P(),
            P("tp", None, None),
            P("tp", None, None),
            P("tp", None),
            P(),
            P("seq", None, "tp"),
            P("seq", None, "tp"),
            P("seq", "tp", None),
            P("seq", None),
            P("seq", None),
        ),
        out_specs=P(("seq", "tp"), None),
        check_vma=False,
    )
```

profile of v0, /device:TPU:1, one launch (start us, length us, event | category | flops | bytes accessed | tf_op | source)
XLA Modules:
  0.0 588.4 jit_solution(11519764345075057940)
XLA Ops:
  6.5 0.0 all-gather.4.cloned.1.call-start
  6.6 16.7 %all_gather.12 = bf16[128,2048]{1,0:T(8,128)(2,1)S(1)} all-gather(bf16[32,2048]{1,0:T(8,128)(2,1)} %param.15), channel_id=1, replica_groups=mesh['seq'=64,'tp'=4] {'tp'}, dimensions={0}, use_global_device_ids=true | all-gather | bytes 655360 | tf_op jit(solution)/shard_map/all_gather | solution.py:78
  23.2 0.2 fusion.38
  23.4 0.6 copy-done.2
  24.0 2.5 fusion.53
  26.6 0.1 multiply_reduce_fusion.1
  26.7 0.8 multiply_convert_fusion
  27.5 0.0 all-gather.4.cloned.1.call-update
  27.5 0.0 all-gather.6.cloned.1.call-start
  27.6 0.1 copy.30
  27.6 0.1 reshape.560
  27.8 1.2 gather_fusion.1
  29.1 0.1 multiply_cosine_fusion
  29.3 0.6 pad_maximum_fusion
  29.9 0.0 all-gather.6.cloned.1.call-update
  29.9 0.0 reduce-scatter.3.cloned.1.call-start
  29.9 0.2 compare_select_fusion
  30.1 1.7 convolution_convert_fusion.3
  31.8 0.2 copy.31
  32.0 0.0 copy-start.9
  32.0 48.9 %gather_fusion = s32[8192]{0:T(1024)S(1)} fusion(s32[128]{0:T(128)S(1)} %reshape.560, s32[8192]{0:T(1024)S(1)} %broadcast_clamp_fusion), kind=kCustom, calls=%fused_computation | custom fusion | bytes 98304 | tf_op jit(solution)/shard_map/gather | solution.py:42
  80.9 0.6 broadcast_compare_fusion
  81.6 0.1 broadcast_multiply_fusion
  81.6 0.1 copy.37
  81.7 0.1 eq.35
  81.9 85.4 %all-gather.4.cloned.1.call-done = bf16[8192,512]{0,1:T(8,128)(2,1)} async-done(((bf16[128,512]{0,1:T(8,128)(2,1)}), bf16[8192,512]{0,1:T(8,128)(2,1)}) %all-gather.4.cloned.1.call-update) | async-done | bytes 8388624 | tf_op jit(solution)/shard_map/all_gather | solution.py:93
  167.3 10.5 %fusion.5 = f32[128,4,8192]{2,0,1:T(8,128)} fusion(bf16[8192,512]{0,1:T(8,128)(2,1)} %all-gather.4.cloned.1.call-done, bf16[4,512,128]{2,1,0:T(8,128)(2,1)S(1)} %copy-done.6, bf16[128,4,192]{0,2,1:T(8,128)(2,1)S(1)} %bitcast.67), kind=kOutput, calls=%fused_computation.11 | convolution fusion | flops 4362338304 | bytes 25821184 | tf_op jit(solution)/shard_map/thl,kl->thk/dot_general | solution.py:97
  177.7 66.1 %all-gather.6.cloned.1.call-done = bf16[8192,64]{0,1:T(8,128)(2,1)} async-done(((bf16[128,64]{0,1:T(8,128)(2,1)}), bf16[8192,64]{0,1:T(8,128)(2,1)}) %all-gather.6.cloned.1.call-update) | async-done | bytes 1048592 | tf_op jit(solution)/shard_map/all_gather | solution.py:94
  243.8 12.0 %fusion.80 = (f32[128,4]{0,1:T(4,128)S(1)}, f32[128,4,8192]{2,0,1:T(8,128)}) fusion(f32[128,4,8192]{2,0,1:T(8,128)} %fusion.5, bf16[8192,64]{0,1:T(8,128)(2,1)} %all-gather.6.cloned.1.call-done, bf16[128,4,32]{0,2,1:T(8,128)(2,1)S(1)} %get-tuple-element.12, bf16[128,4,32]{0,2,1:T(8,128)(2,1)S(1)} %get-tuple-element.11, ...), kind=kOutput, calls=%fused_computation.141 | convolution fusion | flops 553778688 | bytes 35719168 | tf_op jit(solution)/shard_map/thr,kr->thk/dot_general | solution.py:100
  255.8 9.5 %fusion = f32[128,4]{0,1:T(4,128)S(1)} fusion(f32[128,4,8192]{2,0,1:T(8,128)} %get-tuple-element.18, f32[128,4]{0,1:T(4,128)S(1)} %broadcast_maximum_fusion, pred[128,8192]{1,0:T(8,128)(4,1)S(1)} %broadcast_compare_fusion), kind=kLoop, calls=%fused_computation.7 | loop fusion | flops 12582400 | bytes 17829888 | tf_op jit(solution)/shard_map/reduce_sum | solution.py:108
  265.4 13.1 %fusion.33 = bf16[4,128,128]{1,2,0:T(8,128)(2,1)S(1)} fusion(bf16[4,512,128]{2,1,0:T(8,128)(2,1)} %param.22, bf16[8192,512]{0,1:T(8,128)(2,1)} %all-gather.4.cloned.1.call-done, f32[128,4,8192]{2,0,1:T(8,128)} %get-tuple-element.18, f32[128,4]{0,1:T(4,128)S(1)} %broadcast_maximum_fusion, pred[128,8192]{1,0:T(8,128)(4,1)S(1)} %broadcast_compare_fusion, ...), kind=kOutput, calls=%fused_computation.34 | convolution fusion | flops 4375248896 | bytes 26873856 | tf_op jit(solution)/shard_map/thl,hlv->thv/dot_general | solution.py:118
  278.5 1.3 convolution_convert_fusion.1
  279.7 0.0 reduce-scatter.3.cloned.1.call-update
  279.7 0.0 all-gather.8.cloned.1.call-start
  279.8 0.8 reduce-window.6
  280.7 0.2 slice_reduce_fusion
  280.9 0.1 copy.36
  281.0 0.1 mul.267
  281.1 0.1 bitcast_bitcast_fusion
  281.3 19.1 %reduce-scatter.3.cloned.1.call-done = bf16[32,2048]{1,0:T(8,128)(2,1)} async-done(((bf16[128,2048]{1,0:T(8,128)(2,1)}), bf16[32,2048]{1,0:T(8,128)(2,1)}) %reduce-scatter.3.cloned.1.call-update) | async-done | bytes 131088 | tf_op jit(solution)/shard_map/reduce_scatter | solution.py:136
  300.4 1.1 fusion.49
  301.5 1.0 fusion.51
  302.5 4.5 scatter_custom_fusion
  307.0 0.4 reshape.565
  307.5 37.8 %all_to_all.10 = bf16[64,4,2048]{2,1,0:T(4,128)(2,1)} all-to-all(bf16[64,4,2048]{2,1,0:T(4,128)(2,1)S(1)} %reshape.565), channel_id=1, replica_groups=mesh['seq'=64,'tp'=4] {'seq'}, dimensions={0} | all-to-all | bytes 2097152 | tf_op jit(solution)/shard_map/all_to_all | solution.py:149
  345.2 0.0 all-gather.8.cloned.1.call-update
  345.3 0.0 copy-start.13
  345.3 0.0 reduce-scatter.5.cloned.1.call-start
  345.3 84.0 %all-gather.8.cloned.1.call-done = bf16[256,4,2048]{2,1,0:T(4,128)(2,1)} async-done(((bf16[64,4,2048]{2,1,0:T(4,128)(2,1)}), bf16[256,4,2048]{2,1,0:T(4,128)(2,1)}) %all-gather.8.cloned.1.call-update) | async-done | bytes 4194320 | tf_op jit(solution)/shard_map/all_gather | solution.py:150
  429.3 6.9 %reshape.566 = bf16[1024,2048]{1,0:T(8,128)(2,1)} reshape(bf16[256,4,2048]{2,1,0:T(4,128)(2,1)} %all-gather.8.cloned.1.call-done) | data formatting | bytes 8388608 | tf_op jit(solution)/shard_map/reshape | solution.py:151
  436.2 5.2 fusion.12
  441.4 9.0 %convolution_convert_fusion = bf16[1024,2048]{1,0:T(8,128)(2,1)} fusion(bf16[1,352,2048]{2,1,0:T(8,128)(2,1)S(1)} %copy-done.14, bf16[1024,2048]{1,0:T(8,128)(2,1)} %reshape.566, bf16[1,2048,352]{1,2,0:T(8,128)(2,1)} %param.26, f32[1024,352]{0,1:T(8,128)} %fusion.12), kind=kOutput, calls=%fused_computation.16 | convolution fusion | flops 2957049856 | bytes 12713984 | tf_op jit(solution)/shard_map/dot_general | solution.py:162
  450.4 0.0 reduce-scatter.5.cloned.1.call-update
  450.4 82.0 %reduce-scatter.5.cloned.1.call-done = bf16[256,2048]{1,0:T(8,128)(2,1)} async-done(((bf16[1024,2048]{1,0:T(8,128)(2,1)}), bf16[256,2048]{1,0:T(8,128)(2,1)}) %reduce-scatter.5.cloned.1.call-update) | async-done | bytes 1048592 | tf_op jit(solution)/shard_map/reduce_scatter | solution.py:161
  532.5 2.3 reshape.567
  534.7 12.4 %all-to-all-start.1 = ((bf16[64,4,2048]{2,1,0:T(4,128)(2,1)}), bf16[64,4,2048]{2,1,0:T(4,128)(2,1)S(1)}, u32[]{:S(2)}, u32[]{:S(2)}) async-start(bf16[64,4,2048]{2,1,0:T(4,128)(2,1)} %reshape.567), calls=%async_computation.3 | async-start | bytes 2097152 | tf_op jit(solution)/shard_map/all_to_all | solution.py:168
  547.2 0.1 constant_dynamic-slice_fusion
  547.3 0.1 copy.40
  547.4 23.4 %all-to-all-done.1 = bf16[64,4,2048]{2,1,0:T(4,128)(2,1)S(1)} async-done(((bf16[64,4,2048]{2,1,0:T(4,128)(2,1)}), bf16[64,4,2048]{2,1,0:T(4,128)(2,1)S(1)}, u32[]{:S(2)}, u32[]{:S(2)}) %all-to-all-start.1) | async-done | bytes 1048608 | tf_op jit(solution)/shard_map/all_to_all | solution.py:168
  570.8 1.1 reshape.568
  571.9 4.3 gather_fusion.2
  576.2 2.5 reshape.570
  578.8 2.3 multiply_reduce_fusion
  581.1 0.7 fusion.52
  (48 shorter events, 0.3 us)
Async XLA Ops:
  6.5 23.6 %copy-start = (bf16[2048,768]{1,0:T(8,128)(2,1)S(1)}, bf16[2048,768]{1,0:T(8,128)(2,1)}, u32[]{:S(2)}) copy-start(bf16[2048,768]{1,0:T(8,128)(2,1)} %param.18) | copy-start | bytes 9437188
  6.5 23.6 %copy-start.7 = (f32[2048]{0:T(1024)S(1)}, f32[2048]{0:T(1024)}, u32[]{:S(2)}) copy-start(f32[2048]{0:T(1024)} %param.17) | copy-start | bytes 24580
  6.5 20.1 %copy-start.11 = (f32[512]{0:T(512)S(1)}, f32[512]{0:T(512)}, u32[]{:S(2)}) copy-start(f32[512]{0:T(512)} %param.20) | copy-start | bytes 6148
  6.5 21.0 %copy-start.12 = (s32[64,2]{0,1:T(2,128)S(1)}, s32[64,2]{0,1:T(2,128)}, u32[]{:S(2)}) copy-start(s32[64,2]{0,1:T(2,128)} %param.16) | copy-start | bytes 1540
  6.5 160.7 %all-gather.4.cloned.1.call-start = ((), (), s32[]{:S(2)}) async-start(), calls=%async_computation.4 | async-start | bytes 8519680 | tf_op jit(solution)/shard_map/all_gather | solution.py:93
  23.2 0.8 copy-start.2
  27.5 216.3 %all-gather.6.cloned.1.call-start = ((), (), s32[]{:S(2)}) async-start(), calls=%async_computation.5 | async-start | bytes 1064960 | tf_op jit(solution)/shard_map/all_gather | solution.py:94
  29.9 270.5 %reduce-scatter.3.cloned.1.call-start = ((), (), s32[]{:S(2)}) async-start(), calls=%async_computation.6 | async-start | bytes 655360 | tf_op jit(solution)/shard_map/reduce_scatter | solution.py:136
  32.0 49.6 %copy-start.9 = (s32[128,6]{0,1:T(8,128)S(1)}, s32[128,6]{0,1:T(8,128)}, u32[]{:S(2)}) copy-start(s32[128,6]{0,1:T(8,128)} %param.28) | copy-start | bytes 9220
  32.0 135.3 %copy-start.6 = (bf16[4,512,128]{2,1,0:T(8,128)(2,1)S(1)}, bf16[4,512,128]{2,1,0:T(8,128)(2,1)}, u32[]{:S(2)}) copy-start(bf16[4,512,128]{2,1,0:T(8,128)(2,1)} %param.21) | copy-start | bytes 1572868
  265.3 13.1 %copy-start.4 = (bf16[512,2048]{1,0:T(8,128)(2,1)S(1)}, bf16[512,2048]{1,0:T(8,128)(2,1)}, u32[]{:S(2)}) copy-start(bf16[512,2048]{1,0:T(8,128)(2,1)} %param.23) | copy-start | bytes 6291460
  265.3 35.1 %copy-start.3 = (bf16[32,2048]{1,0:T(8,128)(2,1)S(1)}, bf16[32,2048]{1,0:T(8,128)(2,1)}, u32[]{:S(2)}) copy-start(bf16[32,2048]{1,0:T(8,128)(2,1)} %param.15) | copy-start | bytes 393220
  265.4 36.1 %copy-start.8 = (f32[2048]{0:T(1024)S(1)}, f32[2048]{0:T(1024)}, u32[]{:S(2)}) copy-start(f32[2048]{0:T(1024)} %param.24) | copy-start | bytes 24580
  279.7 149.6 %all-gather.8.cloned.1.call-start = ((), (), s32[]{:S(2)}) async-start(), calls=%async_computation.7 | async-start | bytes 5242880 | tf_op jit(solution)/shard_map/all_gather | solution.py:150
  345.3 91.0 %copy-start.13 = (bf16[1,2048,352]{1,2,0:T(8,128)(2,1)S(1)}, bf16[1,2048,352]{1,2,0:T(8,128)(2,1)}, u32[]{:S(2)}) copy-start(bf16[1,2048,352]{1,2,0:T(8,128)(2,1)} %param.25) | copy-start | bytes 4325380
  345.3 187.2 %reduce-scatter.5.cloned.1.call-start = ((), (), s32[]{:S(2)}) async-start(), calls=%async_computation.8 | async-start | bytes 5242880 | tf_op jit(solution)/shard_map/reduce_scatter | solution.py:161
  436.2 5.2 copy-start.14
  450.4 96.8 %copy-start.10 = (f32[128,6]{0,1:T(8,128)S(1)}, f32[128,6]{0,1:T(8,128)}, u32[]{:S(2)}) copy-start(f32[128,6]{0,1:T(8,128)} %param.29) | copy-start | bytes 9220
  534.7 36.1 %all-to-all-start.1 = ((bf16[64,4,2048]{2,1,0:T(4,128)(2,1)}), bf16[64,4,2048]{2,1,0:T(4,128)(2,1)S(1)}, u32[]{:S(2)}, u32[]{:S(2)}) async-start(bf16[64,4,2048]{2,1,0:T(4,128)(2,1)} %reshape.567), calls=%async_computation.3 | async-start | bytes 2097152 | tf_op jit(solution)/shard_map/all_to_all | solution.py:168
  571.9 9.9 %copy-start.1 = (bf16[2048,768]{1,0:T(8,128)(2,1)S(1)}, bf16[2048,768]{1,0:T(8,128)(2,1)}, u32[]{:S(2)}) copy-start(bf16[2048,768]{1,0:T(8,128)(2,1)} %param.18) | copy-start | bytes 9437188
  576.2 4.9 copy-start.5
Sparse Core Ops, SparseCore 0:
  27.6 139.5 all-gather.3
  170.6 73.1 all-gather.5
  279.9 20.4 reduce-scatter.2
  345.4 83.8 all-gather.7
  450.6 81.8 reduce-scatter.4
where the time goes:
time: 594 us; the launch traced here: 588 us
  waiting for transfers between devices  360 us (61%)
  local copies, waits for them, and re-layouts  74 us (12%)
  matrix products  55.2 us (9%)
  blocking collectives  54.4 us (9%)
  other arithmetic  18.5 us (3%)
  between operations  13.5 us (2%)
  starting transfers between devices  12.6 us (2%)
    all_gather x1, waiting for transfers between devices, body(): piece_latent = lax.all_gather(latent, 'seq', axis=0, tiled=True)  85.4 us
    all_gather x1, waiting for transfers between devices, body(): piece_data = lax.all_gather(arrived, 'tp', axis=0, tiled=True)  84 us
    reduce_scatter x1, waiting for transfers between devices, body(): lax.psum_scatter(jnp.dot(hidden, down_local, preferred_element_type=jnp.f...  82 us
    all_gather x1, waiting for transfers between devices, body(): piece_rope = lax.all_gather(key_rope, 'seq', axis=0, tiled=True)  66.1 us
    gather x2, local copies, waits for them, and re-layouts, positions(): block_num = block_ids.reshape(-1)[device * 2 + within // half_width]  50.1 us
    all_to_all x1, blocking collectives, body(): lax.all_to_all(packed, 'seq', split_axis=0, concat_axis=0, tiled=True)  37.8 us
    all_to_all x1, waiting for transfers between devices, body(): lax.all_to_all(expert_out, 'seq', split_axis=0, concat_axis=0, tiled=True)  23.4 us
    reduce_scatter x1, waiting for transfers between devices, body(): lax.psum_scatter(partial_out.astype(jnp.bfloat16), 'tp', scatter_dimensio...  19.1 us
  transfers between devices with their start and end apart: 6, of which 6 were waited for; matrix products, arithmetic and copies ran while one was open for 11% of the time, Pallas kernels for 0%

commit v1 on v0

v1 whole, which is shorter than its diff:
```python
import functools
import math

import jax
import jax.numpy as jnp
from jax import lax
from jax.experimental import pallas as pl
from jax.experimental.pallas import tpu as pltpu
from jax.sharding import PartitionSpec as P

EPSILON = 1e-06
MESH = pl.DeviceIdType.MESH
BF = jnp.bfloat16
F32 = jnp.float32
KEYW = 640


def place():
    s = lax.axis_index("seq")
    t = lax.axis_index("tp")
    return (s // 32) * 4 + t, (s // 8) % 4, (s // 2) % 4, s % 2


def dev(z, y, x, c):
    z, y, x, c = z % 8, y % 4, x % 4, c % 2
    return ((z // 4) * 32 + y * 8 + x * 2 + c, z % 4)


def greet(peers):
    barrier = pltpu.get_barrier_semaphore()
    for p in peers:
        pl.semaphore_signal(barrier, inc=1, device_id=p, device_id_type=MESH)
    pl.semaphore_wait(barrier, len(peers))


def rcopy(src, dst, ss, rs, device):
    return pltpu.make_async_remote_copy(
        src_ref=src, dst_ref=dst, send_sem=ss, recv_sem=rs, device_id=device, device_id_type=MESH
    )


def normalize(values, gain_vec):
    values = values.astype(F32)
    factor = lax.rsqrt(jnp.mean(values * values, axis=-1, keepdims=True) + EPSILON)
    return values * factor * gain_vec


def rotate(values, position):
    half_width = values.shape[-1] // 2
    frequency = jnp.exp(
        jnp.arange(half_width, dtype=F32) * (-2.0 * math.log(10000.0) / values.shape[-1])
    )
    angles = position.astype(F32).reshape(position.shape + (1,) * (values.ndim - 1)) * frequency
    cosine = jnp.cos(angles)
    sine_part = jnp.sin(angles)
    first_half = values[..., :half_width]
    second_half = values[..., half_width:]
    return jnp.concatenate(
        [
            first_half * cosine - second_half * sine_part,
            second_half * cosine + first_half * sine_part,
        ],
        axis=-1,
    )


def gather_kernel(kv_ref, nt_ref, rg_ref, KV, NT, RG, ssem, rsem, lsem):
    z, y, x, c = place()
    zh, t = z // 4, z % 4
    peers = [dev(z + k, y, x, c) for k in range(1, 8)]
    xs = [dev(z, y, x + 1, c), dev(z, y, x + 3, c)]
    ys = [dev(z, y + 1, x, c), dev(z, y + 3, x, c)]
    other = dev(z, y, x, c + 1)
    greet(peers + xs + ys + [other])
    number = [0]
    sent = []

    def send(src, dst, device):
        i = number[0]
        number[0] += 1
        cp = rcopy(src, dst, ssem.at[i], rsem.at[i], device)
        cp.start()
        sent.append(cp)
        return i

    def arrived(i, region):
        rcopy(region, region, ssem.at[i], rsem.at[i], other).wait_recv()

    rows = pl.ds(pl.multiple_of(t * 32, 32), 32)
    zi = {}
    mine = KV.at[zh, y, x, c, rows]
    for k in (4, 3, 5, 2, 6, 1, 7):
        zi[k] = send(kv_ref, mine, dev(z + k, y, x, c))
    locals_ = [
        pltpu.make_async_copy(kv_ref, mine, lsem.at[0]),
        pltpu.make_async_copy(nt_ref, NT.at[t], lsem.at[1]),
        pltpu.make_async_copy(rg_ref, RG.at[zh], lsem.at[2]),
    ]
    for cp in locals_:
        cp.start()
    ri = send(rg_ref, RG.at[zh], dev(z + 4, y, x, c))
    ti = {}
    for k in (3, 2, 1):
        ti[k] = send(nt_ref, NT.at[t], (zh * 32 + y * 8 + x * 2 + c, (t + k) % 4))
    for cp in locals_:
        cp.wait()
    for k in zi:
        zz = (z - k + 8) % 8
        arrived(zi[k], KV.at[zz // 4, y, x, c, pl.ds(pl.multiple_of((zz % 4) * 32, 32), 32)])
    lo, hi = pl.ds(0, 64), pl.ds(64, 64)
    xm, xp, xo = (x + 3) % 4, (x + 1) % 4, (x + 2) % 4
    ym, yp, yo = (y + 3) % 4, (y + 1) % 4, (y + 2) % 4
    a, b = KV.at[0, y, x, c], KV.at[1, y, x, c]
    ap = send(a, a, xs[0])
    am = send(a, a, xs[1])
    bp = send(b, b, ys[0])
    bm = send(b, b, ys[1])
    arrived(ap, KV.at[0, y, xm, c])
    g = KV.at[0, y, xm, c, lo]
    ap2 = send(g, g, xs[0])
    arrived(bp, KV.at[1, ym, x, c])
    g = KV.at[1, ym, x, c, lo]
    bp2 = send(g, g, ys[0])
    arrived(am, KV.at[0, y, xp, c])
    g = KV.at[0, y, xp, c, hi]
    am2 = send(g, g, xs[1])
    arrived(bm, KV.at[1, yp, x, c])
    g = KV.at[1, yp, x, c, hi]
    bm2 = send(g, g, ys[1])
    arrived(ap2, KV.at[0, y, xo, c, lo])
    arrived(am2, KV.at[0, y, xo, c, hi])
    r = KV.at[0, y, :, c]
    rp = send(r, r, ys[0])
    rm = send(r, r, ys[1])
    arrived(bp2, KV.at[1, yo, x, c, lo])
    arrived(bm2, KV.at[1, yo, x, c, hi])
    q = KV.at[1, :, x, c]
    qp = send(q, q, xs[0])
    qm = send(q, q, xs[1])
    across = [send(r, r, other), send(q, q, other)]
    arrived(rp, KV.at[0, ym, :, c])
    g = KV.at[0, ym, :, c, lo]
    rp2 = send(g, g, ys[0])
    arrived(qp, KV.at[1, :, xm, c])
    g = KV.at[1, :, xm, c, lo]
    qp2 = send(g, g, xs[0])
    arrived(rm, KV.at[0, yp, :, c])
    g = KV.at[0, yp, :, c, hi]
    rm2 = send(g, g, ys[1])
    arrived(qm, KV.at[1, :, xp, c])
    g = KV.at[1, :, xp, c, hi]
    qm2 = send(g, g, xs[1])
    for g in (KV.at[0, ym, :, c], KV.at[1, :, xm, c], KV.at[0, yp, :, c], KV.at[1, :, xp, c]):
        across.append(send(g, g, other))
    arrived(rp2, KV.at[0, yo, :, c, lo])
    arrived(rm2, KV.at[0, yo, :, c, hi])
    g = KV.at[0, yo, :, c]
    across.append(send(g, g, other))
    arrived(qp2, KV.at[1, :, xo, c, lo])
    arrived(qm2, KV.at[1, :, xo, c, hi])
    g = KV.at[1, :, xo, c]
    across.append(send(g, g, other))
    d = 1 - c
    for i, region in zip(
        across,
        (
            KV.at[0, y, :, d],
            KV.at[1, :, x, d],
            KV.at[0, ym, :, d],
            KV.at[1, :, xm, d],
            KV.at[0, yp, :, d],
            KV.at[1, :, xp, d],
            KV.at[0, yo, :, d],
            KV.at[1, :, xo, d],
        ),
    ):
        arrived(i, region)
    for k in ti:
        arrived(ti[k], NT.at[(t - k + 4) % 4])
    arrived(ri, RG.at[1 - zh])
    for cp in sent:
        cp.wait_send()


def gather_keys(kv_own, normed_own, rg):
    count = 40
    vm = pl.BlockSpec(memory_space=pltpu.VMEM)
    return pl.pallas_call(
        gather_kernel,
        out_shape=(
            jax.ShapeDtypeStruct((2, 4, 4, 2, 128, KEYW), BF),
            jax.ShapeDtypeStruct((4, 32, 2048), BF),
            jax.ShapeDtypeStruct((2, 16, 128), F32),
        ),
        in_specs=[vm, vm, vm],
        out_specs=(pl.BlockSpec(memory_space=pl.ANY), vm, vm),
        scratch_shapes=[
            pltpu.SemaphoreType.DMA((count,)),
            pltpu.SemaphoreType.DMA((count,)),
            pltpu.SemaphoreType.DMA((3,)),
        ],
        compiler_params=pltpu.CompilerParams(
            collective_id=0, has_side_effects=True, vmem_limit_bytes=16 * 2**20
        ),
        name="gather_keys",
    )(kv_own, normed_own, rg)


CHUNK = 512


def attention_kernel(inv_ref, blk_ref, q_ref, kv_hbm, o_ref, kbuf, m_ref, l_ref, acc_ref, sems):
    low = blk_ref[0]
    per = CHUNK // 64
    top_chunks = (127 - low) // per + 1

    def fetch(p, start):
        second = p >= 64
        d = inv_ref[jnp.where(second, 127 - p, p)]
        off = pl.multiple_of(jnp.where(second, 64, 0), 64)
        cp = pltpu.make_async_copy(
            kv_hbm.at[d, pl.ds(off, 64)],
            kbuf.at[pl.ds(pl.multiple_of(p * 64, 64), 64)],
            sems.at[p // per],
        )
        cp.start()

    def issue(p, carry):
        fetch(p, True)
        return carry

    lax.fori_loop(0, top_chunks * per, issue, 0)
    scale = (128 + 64) ** (-0.5)

    for half in (1, 0):
        block = low if half == 0 else 127 - low
        last = block // per
        m_ref[...] = jnp.full_like(m_ref, -1e30)
        l_ref[...] = jnp.zeros_like(l_ref)
        acc_ref[...] = jnp.zeros_like(acc_ref)

        def step(ch, masked):
            region = kbuf.at[pl.ds(pl.multiple_of(ch * CHUNK, CHUNK), CHUNK)]
            if half == 1:
                pltpu.make_async_copy(region, region, sems.at[ch]).wait()
            keys = region[...]
            s = lax.dot_general(
                q_ref[half], keys, (((1,), (1,)), ((), ())), preferred_element_type=F32
            )
            s = s * scale
            if masked:
                row = lax.broadcasted_iota(jnp.int32, s.shape, 0) % 64
                col = lax.broadcasted_iota(jnp.int32, s.shape, 1)
                s = jnp.where(col - row <= block * 64 - ch * CHUNK, s, -1e30)
            m_old = m_ref[...]
            m_new = jnp.maximum(m_old, jnp.max(s, axis=1, keepdims=True))
            p = jnp.exp(s - m_new)
            alpha = jnp.exp(m_old - m_new)
            l_ref[...] = l_ref[...] * alpha + jnp.sum(p, axis=1, keepdims=True)
            acc_ref[...] = acc_ref[...] * alpha + jnp.dot(
                p.astype(BF), keys[:, :512], preferred_element_type=F32
            )
            m_ref[...] = m_new

        def loop(ch, carry):
            step(ch, False)
            return carry

        lax.fori_loop(0, last, loop, 0)
        step(last, True)
        o_ref[half] = (acc_ref[...] / l_ref[...]).astype(BF)


def attention(inv, low, q, kv):
    return pl.pallas_call(
        attention_kernel,
        out_shape=jax.ShapeDtypeStruct((2, 256, 512), BF),
        in_specs=[
            pl.BlockSpec(memory_space=pltpu.SMEM),
            pl.BlockSpec(memory_space=pltpu.SMEM),
            pl.BlockSpec(memory_space=pltpu.VMEM),
            pl.BlockSpec(memory_space=pl.ANY),
        ],
        out_specs=pl.BlockSpec(memory_space=pltpu.VMEM),
        scratch_shapes=[
            pltpu.VMEM((8192, KEYW), BF),
            pltpu.VMEM((256, 1), F32),
            pltpu.VMEM((256, 1), F32),
            pltpu.VMEM((256, 512), F32),
            pltpu.SemaphoreType.DMA((8192 // CHUNK,)),
        ],
        compiler_params=pltpu.CompilerParams(vmem_limit_bytes=32 * 2**20),
        name="attention",
    )(inv, low, q, kv)


def tp_scatter_kernel(p_ref, o_ref, ssem, rsem, lsem):
    z, y, x, c = place()
    s, t = lax.axis_index("seq"), lax.axis_index("tp")
    greet([(s, (t + k) % 4) for k in (1, 2, 3)])
    cps = []
    for k in (2, 3, 1):
        to = (t + k) % 4
        cp = rcopy(p_ref.at[to], o_ref.at[k], ssem.at[k], rsem.at[k], (s, to))
        cp.start()
        cps.append(cp)
    own = pltpu.make_async_copy(p_ref.at[t], o_ref.at[0], lsem)
    own.start()
    own.wait()
    for cp in cps:
        cp.wait()


def column_kernel(scatter, p_ref, o_ref, ssem, rsem, lsem):
    z, y, x, c = place()
    greet([dev(z + k, y, x, c) for k in range(1, 8)])
    cps = []
    for k in (4, 3, 5, 2, 6, 1, 7):
        to = (z + k) % 8
        if scatter:
            cp = rcopy(p_ref.at[to], o_ref.at[k], ssem.at[k], rsem.at[k], dev(to, y, x, c))
        else:
            cp = rcopy(p_ref, o_ref.at[z], ssem.at[k], rsem.at[k], dev(to, y, x, c))
        cp.start()
        cps.append(cp)
    if scatter:
        own = pltpu.make_async_copy(p_ref.at[z], o_ref.at[0], lsem)
    else:
        own = pltpu.make_async_copy(p_ref, o_ref.at[z], lsem)
    own.start()
    own.wait()
    for cp in cps:
        cp.wait()


def exchange(kernel, name, cid, array, out):
    vm = pl.BlockSpec(memory_space=pltpu.VMEM)
    return pl.pallas_call(
        kernel,
        out_shape=jax.ShapeDtypeStruct(out, BF),
        in_specs=[vm],
        out_specs=vm,
        scratch_shapes=[
            pltpu.SemaphoreType.DMA((8,)),
            pltpu.SemaphoreType.DMA((8,)),
            pltpu.SemaphoreType.DMA,
        ],
        compiler_params=pltpu.CompilerParams(
            collective_id=cid, has_side_effects=True, vmem_limit_bytes=16 * 2**20
        ),
        name=name,
    )(array)


def experts_kernel(
    sa, sb, wg, wu, wd, ra, rb, la, lb, xa, xb, oa, ob, ma, mb,
    s1, r1, s2a, r2a, s2b, r2b, s3a, r3a, s3b, r3b, s4, r4, lsem,
):
    z, y, x, c = place()
    peers = [dev(z, y, x, c + 1)]
    for k in (1, 2, 3):
        for d in (0, 1):
            peers.append(dev(z, y + k, x, c + d))
            peers.append(dev(z, y, x + k, c + d))
    greet(peers)

    def blk(j):
        return pl.ds(pl.multiple_of(j * 32, 32), 32)

    hop1a = {}
    hop1b = {}
    for k in (1, 3, 2):
        hop1a[k] = rcopy(sa.at[k], la.at[k], s1.at[k], r1.at[k], dev(z, y, x + k, c))
        hop1b[k] = rcopy(sb.at[k], lb.at[k], s1.at[4 + k], r1.at[4 + k], dev(z, y + k, x, c))
        hop1a[k].start()
        hop1b[k].start()

    def hop2a(k, src, j):
        return rcopy(
            src.at[k, blk(j)], xa.at[k, blk(j)], s2a.at[k, j], r2a.at[k, j],
            dev(z, y + j // 2, x, c + j % 2),
        )

    def hop2b(k, src, j):
        return rcopy(
            src.at[k, blk(j)], xb.at[j // 2, blk(k * 2 + j % 2)], s2b.at[k, j], r2b.at[k, j],
            dev(z, y, x + j // 2, c + j % 2),
        )

    def own2(k, sra, srb):
        return (
            pltpu.make_async_copy(sra.at[k, blk(0)], xa.at[k, blk(0)], lsem.at[k]),
            pltpu.make_async_copy(srb.at[k, blk(0)], xb.at[0, blk(k * 2)], lsem.at[4 + k]),
        )

    for k in (0, 1, 3, 2):
        if k:
            hop1a[k].wait_recv()
            hop1b[k].wait_recv()
        sra, srb = (la, lb) if k else (sa, sb)
        for j in (2, 6, 4, 3, 7, 5, 1):
            hop2a(k, sra, j).start()
            hop2b(k, srb, j).start()
        for cp in own2(k, sra, srb):
            cp.start()
    for k in range(4):
        sra, srb = (la, lb) if k else (sa, sb)
        for cp in own2(k, sra, srb):
            cp.wait()

    def hop3a(k, j, dst):
        return rcopy(
            oa.at[k, blk(j)], dst.at[k, blk(j)], s3a.at[k, j], r3a.at[k, j],
            dev(z, y + 4 - j // 2, x, c + j % 2),
        )

    def hop3b(k, j, dst):
        return rcopy(
            ob.at[k, blk(j)], dst.at[j // 2, blk(k * 2 + j % 2)], s3b.at[k, j], r3b.at[k, j],
            dev(z, y, x + 4 - k, c + j % 2),
        )

    def own3(k):
        return ()

    for k in (0, 1, 3, 2):
        for j in range(1, 8):
            hop2a(k, la, j).wait_recv()
        for i in range(4):
            for d in (0, 1):
                if k or d:
                    hop2b(i, lb, k * 2 + d).wait_recv()
        rows_a = xa[k]
        rows_b = xb[k]
        gate = jnp.dot(rows_a, wg[:1024], preferred_element_type=F32) + jnp.dot(
            rows_b, wg[1024:], preferred_element_type=F32
        )
        up = jnp.dot(rows_a, wu[:1024], preferred_element_type=F32) + jnp.dot(
            rows_b, wu[1024:], preferred_element_type=F32
        )
        hidden = (gate / (1.0 + jnp.exp(-gate)) * up).astype(BF)
        oa[k] = jnp.dot(hidden, wd[:, :1024], preferred_element_type=F32).astype(BF)
        ob[k] = jnp.dot(hidden, wd[:, 1024:], preferred_element_type=F32).astype(BF)
        for j in range(1, 8):
            hop3a(k, j, ma if k else ra).start()
        cp = pltpu.make_async_copy(
            oa.at[k, blk(0)], (ma if k else ra).at[k, blk(0)], lsem.at[8 + k]
        )
        cp.start()
        for j in range(8):
            i = j // 2
            if k or j % 2:
                hop3b(k, j, mb if i else rb).start()
            else:
                pltpu.make_async_copy(
                    ob.at[k, blk(j)], (mb if i else rb).at[i, blk(0)], lsem.at[12 + i]
                ).start()

    hop4 = []
    for k in (1, 3, 2):
        for j in range(1, 8):
            hop3a(k, j, ma).wait_recv()
        pltpu.make_async_copy(oa.at[k, blk(0)], ma.at[k, blk(0)], lsem.at[8 + k]).wait()
        cp = rcopy(ma.at[k], ra.at[k], s4.at[k], r4.at[k], dev(z, y, x + 4 - k, c))
        cp.start()
        hop4.append(cp)
    for i in (1, 3, 2):
        for k in range(4):
            for d in (0, 1):
                if k or d:
                    hop3b(k, i * 2 + d, mb).wait_recv()
        pltpu.make_async_copy(ob.at[0, blk(i * 2)], mb.at[i, blk(0)], lsem.at[12 + i]).wait()
        cp = rcopy(mb.at[i], rb.at[i], s4.at[4 + i], r4.at[4 + i], dev(z, y + 4 - i, x, c))
        cp.start()
        hop4.append(cp)
    for j in range(1, 8):
        hop3a(0, j, ra).wait_recv()
    pltpu.make_async_copy(oa.at[0, blk(0)], ra.at[0, blk(0)], lsem.at[8]).wait()
    for k in range(4):
        for d in (0, 1):
            if k or d:
                hop3b(k, d, rb).wait_recv()
    pltpu.make_async_copy(ob.at[0, blk(0)], rb.at[0, blk(0)], lsem.at[12]).wait()
    for cp in hop4:
        cp.wait()
    for k in (1, 2, 3):
        hop1a[k].wait_send()
        hop1b[k].wait_send()
    for k in range(4):
        for j in range(1, 8):
            hop2a(k, la, j).wait_send()
            hop2b(k, lb, j).wait_send()
            hop3a(k, j, ma).wait_send()
        for j in range(8):
            if k or j % 2:
                hop3b(k, j, mb).wait_send()


def experts(sa, sb, wg, wu, wd):
    vm = pl.BlockSpec(memory_space=pltpu.VMEM)
    big = (4, 256, 1024)
    dma = pltpu.SemaphoreType.DMA
    return pl.pallas_call(
        experts_kernel,
        out_shape=(jax.ShapeDtypeStruct(big, BF), jax.ShapeDtypeStruct(big, BF)),
        in_specs=[vm] * 5,
        out_specs=(vm, vm),
        scratch_shapes=[pltpu.VMEM(big, BF)] * 8
        + [
            dma((8,)), dma((8,)),
            dma((4, 8)), dma((4, 8)), dma((4, 8)), dma((4, 8)),
            dma((4, 8)), dma((4, 8)), dma((4, 8)), dma((4, 8)),
            dma((8,)), dma((8,)),
            dma((16,)),
        ],
        compiler_params=pltpu.CompilerParams(
            collective_id=4, has_side_effects=True, vmem_limit_bytes=56 * 2**20
        ),
        name="experts",
    )(sa, sb, wg, wu, wd)


def slot_tables(routes, gates, z, y, x, c):
    e_dy = lax.broadcasted_iota(jnp.int32, (4, 4, 2), 0)
    e_dx = lax.broadcasted_iota(jnp.int32, (4, 4, 2), 1)
    e_dc = lax.broadcasted_iota(jnp.int32, (4, 4, 2), 2)
    expert = (z // 4) * 32 + ((y + e_dy) % 4) * 8 + ((x + e_dx) % 4) * 2 + (c + e_dc) % 2
    expert = expert.reshape(32)
    hit = routes[:, :, None] == expert[None, None, :]
    member = jnp.any(hit, axis=1)
    gate = jnp.sum(jnp.where(hit, gates[:, :, None], 0.0), axis=1)
    ti = lax.broadcasted_iota(jnp.int32, (256, 256), 0)
    tj = lax.broadcasted_iota(jnp.int32, (256, 256), 1)
    before = ((tj < ti) & (tj // 32 == ti // 32)).astype(BF)
    rank = jnp.dot(before, member.astype(BF), preferred_element_type=F32).astype(jnp.int32)
    token = lax.broadcasted_iota(jnp.int32, (256, 32), 0)
    slot = jnp.where(member, (token // 32) * 4 + rank, -1)
    number = lax.broadcasted_iota(jnp.int32, (32, 32, 256), 1)
    pick = slot.T[:, None, :] == number
    table_b = pick.astype(BF)
    weighted = jnp.where(pick, gate.T[:, None, :], 0.0)
    hi = weighted.astype(BF)
    lo = (weighted - hi.astype(F32)).astype(BF)

    def swap(v):
        return v.reshape(4, 4, 2, 32, 256).transpose(1, 0, 2, 3, 4).reshape(1024, 256)

    flat = lambda v: v.reshape(1024, 256)
    return (swap(table_b), flat(table_b)), ((swap(hi), swap(lo)), (flat(hi), flat(lo)))


def body(
    tokens, block_ids, attn_gain, q_weight, kv_weight, kv_gain, uk_weight, uv_weight,
    o_weight, ffn_gain, w_gate, w_up, w_down, routes, gate_weights,
):
    z, y, x, c = place()
    t = lax.axis_index("tp")
    s = lax.axis_index("seq")
    own_blocks = lax.dynamic_slice(block_ids, (s, 0), (1, 2))[0]
    normed_own = normalize(tokens, attn_gain).astype(BF)
    own_pos = own_blocks[t // 2] * 64 + (t % 2) * 32 + jnp.arange(32, dtype=jnp.int32)
    projected = jnp.dot(normed_own, kv_weight, preferred_element_type=F32)
    latent = normalize(projected[:, :512], kv_gain).astype(BF)
    key_rope = rotate(projected[:, 512:], own_pos).astype(BF)
    kv_own = jnp.concatenate([latent, key_rope, jnp.zeros((32, 64), BF)], axis=1)
    pad2 = jnp.zeros((2, 128), F32)
    rg = jnp.concatenate([routes.astype(F32).T, pad2, gate_weights.T, pad2], axis=0)
    kv, normed, rgs = gather_keys(kv_own, normed_own, rg)

    normed = normed.reshape(128, 2048)
    query_pos = (own_blocks[:, None] * 64 + jnp.arange(64, dtype=jnp.int32)[None, :]).reshape(128)
    queries = jnp.dot(normed, q_weight, preferred_element_type=F32).astype(BF)
    queries = queries.reshape(128, 4, 192)
    query_rope = rotate(queries[..., 128:].astype(F32), query_pos).astype(BF)
    query_latent = jnp.einsum(
        "thn,hln->htl", queries[..., :128], uk_weight, preferred_element_type=F32
    ).astype(BF)
    q = jnp.concatenate(
        [query_latent, query_rope.transpose(1, 0, 2), jnp.zeros((4, 128, 64), BF)], axis=2
    )
    q = q.reshape(4, 2, 64, KEYW).transpose(1, 0, 2, 3).reshape(2, 256, KEYW)
    ids = jnp.arange(64, dtype=jnp.int32)
    inv = jnp.sum(
        jnp.where(block_ids[:, 0][None, :] == ids[:, None], ids[None, :], 0), axis=1
    ).astype(jnp.int32)
    out_latent = attention(inv, own_blocks[:1], q, kv.reshape(64, 128, KEYW))
    out_latent = out_latent.reshape(2, 4, 64, 512).transpose(1, 0, 2, 3).reshape(4, 128, 512)
    head_out = jnp.einsum(
        "htl,hlv->thv", out_latent, uv_weight, preferred_element_type=F32
    ).astype(BF)
    partial_out = jnp.dot(head_out.reshape(128, 512), o_weight, preferred_element_type=F32)
    parts = exchange(
        tp_scatter_kernel, "tp_scatter", 1, partial_out.astype(BF).reshape(4, 32, 2048),
        (4, 32, 2048),
    )
    attn_own = jnp.sum(parts.astype(F32), axis=0)
    mixed = (tokens.astype(F32) + attn_own).astype(BF)
    normed_ffn = normalize(mixed, ffn_gain).astype(BF)
    column = exchange(
        functools.partial(column_kernel, False), "column_gather", 2, normed_ffn, (8, 32, 2048)
    ).reshape(256, 2048)

    all_routes = rgs[:, :6].transpose(0, 2, 1).reshape(256, 6).astype(jnp.int32)
    all_gates = rgs[:, 8:14].transpose(0, 2, 1).reshape(256, 6)
    (pa, pb), (ca, cb) = slot_tables(all_routes, all_gates, z, y, x, c)
    sa = jnp.dot(pa, column[:, :1024], preferred_element_type=F32).astype(BF)
    sb = jnp.dot(pb, column[:, 1024:], preferred_element_type=F32).astype(BF)
    ra, rb = experts(
        sa.reshape(4, 256, 1024), sb.reshape(4, 256, 1024), w_gate[0], w_up[0], w_down[0]
    )

    def combine(tables, returned):
        returned = returned.reshape(1024, 1024)
        hi, lo = tables
        dims = (((0,), (0,)), ((), ()))
        return lax.dot_general(hi, returned, dims, preferred_element_type=F32) + lax.dot_general(
            lo, returned, dims, preferred_element_type=F32
        )

    combined = jnp.concatenate([combine(ca, ra), combine(cb, rb)], axis=1).astype(BF)
    sums = exchange(
        functools.partial(column_kernel, True), "column_scatter", 3,
        combined.reshape(8, 32, 2048), (8, 32, 2048),
    )
    return (mixed.astype(F32) + jnp.sum(sums.astype(F32), axis=0)).astype(BF)


def solution(mesh):
    return jax.shard_map(
        body,
        mesh=mesh,
        in_specs=(
            P(("seq", "tp"), None), P(), P(), P(None, "tp"), P(), P(),
            P("tp", None, None), P("tp", None, None), P("tp", None), P(),
            P("seq", None, "tp"), P("seq", None, "tp"), P("seq", "tp", None),
            P("seq", None), P("seq", None),
        ),
        out_specs=P(("seq", "tp"), None),
        check_vma=False,
    )
```

time: 594 us -> 318 us (0.54)
  waiting for transfers between devices: 360 us -> 0 us
  Pallas kernels: 0 us -> 272 us
  blocking collectives: 54.4 us -> 0 us
  local copies, waits for them, and re-layouts: 74 us -> 20.4 us
  matrix products: 55.2 us -> 16.4 us
  starting transfers between devices: 12.6 us -> 0 us
  between operations: 13.5 us -> 1.26 us
  other arithmetic: 18.5 us -> 7.7 us
    pallas_call x0 -> x6, Pallas kernels: none -> 272 us  [the longest x1 117 us: experts(): pl.pallas_call(experts_kernel, out_shape=(jax.ShapeDtypeStruct(big, BF),...]
    all_gather x3 -> x0, waiting for transfers between devices: 235 us -> none  [the longest x1 85.4 us: body(): piece_latent = lax.all_gather(latent, 'seq', axis=0, tiled=True)]
    reduce_scatter x2 -> x0, waiting for transfers between devices: 101 us -> none  [the longest x1 82 us: body(): lax.psum_scatter(jnp.dot(hidden, down_local, preferred_element_type=jnp.f...]
    gather x3 -> x0, local copies, waits for them, and re-layouts: 54.4 us -> none  [the longest x2 50.1 us: positions(): block_num = block_ids.reshape(-1)[device * 2 + within // half_width]]
    dot_general x8 -> x12, matrix products: 55.2 us -> 16.4 us  [the longest x2 3.19 us: combine(): lax.dot_general(hi, returned, dims, preferred_element_type=F32)]
    all_to_all x1 -> x0, blocking collectives: 37.8 us -> none  [body(): lax.all_to_all(packed, 'seq', split_axis=0, concat_axis=0, tiled=True)]
    all_to_all x1 -> x0, waiting for transfers between devices: 23.4 us -> none  [body(): lax.all_to_all(expert_out, 'seq', split_axis=0, concat_axis=0, tiled=True)]
    all_gather x1 -> x0, blocking collectives: 16.7 us -> none  [body(): all_tokens = lax.all_gather(tokens, 'tp', axis=0, tiled=True)]
  transfers between devices with their start and end apart: 6 -> 0, of which waited for: 6 -> 0; matrix products, arithmetic and copies ran while one was open for 11% -> 0% of each run, Pallas kernels for 0% -> 0%
where the time goes in v1:
time: 318 us; the launch traced here: 317 us
  Pallas kernels  272 us (86%)
  local copies, waits for them, and re-layouts  20.4 us (6%)
  matrix products  16.4 us (5%)
  other arithmetic  7.7 us (2%)
    pallas_call x1, Pallas kernels, experts(): pl.pallas_call(experts_kernel, out_shape=(jax.ShapeDtypeStruct(big, BF),...  117 us
    pallas_call x3, Pallas kernels, exchange(): pl.pallas_call(kernel, out_shape=jax.ShapeDtypeStruct(out, BF), in_specs=...  72.3 us
    pallas_call x1, Pallas kernels, gather_keys(): pl.pallas_call(gather_kernel, out_shape=(jax.ShapeDtypeStruct((2, 4, 4, 2...  54.8 us
    pallas_call x1, Pallas kernels, attention(): pl.pallas_call(attention_kernel, out_shape=jax.ShapeDtypeStruct((2, 256,...  27.9 us
    unnamed x39, local copies, waits for them, and re-layouts  17.4 us

profile of v1, /device:TPU:1, one launch (start us, length us, event | category | flops | bytes accessed | tf_op | source)
XLA Modules:
  0.0 317.4 jit_solution(4272521950880245935)
XLA Ops:
  0.0 1.4 dynamic_slice.7
  2.1 1.0 fusion.8
  3.2 1.0 fusion.10.nt_ref
  4.2 2.4 fusion.43
  6.7 0.1 fusion.31
  6.8 0.1 multiply_reduce_fusion
  7.0 0.1 multiply_convert_fusion
  7.0 0.2 copy-done.16
  7.2 0.1 pad.14.clone
  7.3 0.1 maximum_maximum_fusion.1.kv_ref
  7.4 0.5 copy-done.10
  7.9 54.8 %gather_keys.1 = (bf16[2,4,4,2,128,640]{5,4,3,2,1,0:T(8,128)(2,1)S(1)}, bf16[4,32,2048]{2,1,0:T(8,128)(2,1)S(1)}, f32[2,16,128]{2,1,0:T(8,128)S(1)}) custom-call(bf16[32,640]{1,0:T(8,128)(2,1)S(1)} %maximum_maximum_fusion.1.kv_ref, bf16[32,2048]{1,0:T(8,128)(2,1)S(1)} %fusion.10.nt_ref, f32[16,128]{1,0:T(8,128)S(1)} %pad_maximum_fusion.1.rg_ref), custom_call_target="tpu_custom_call" | custom-call | tf_op jit(solution)/shard_map/gather_keys/pallas_call | solution.py:188
  62.7 4.0 %copy-done.1 = bf16[2,4,4,2,128,640]{5,4,3,2,1,0:T(8,128)(2,1)} copy-done((bf16[2,4,4,2,128,640]{5,4,3,2,1,0:T(8,128)(2,1)}, bf16[2,4,4,2,128,640]{5,4,3,2,1,0:T(8,128)(2,1)S(1)}, u32[]{:S(2)}) %copy-start.1) | copy-done | bytes 10485784
  66.7 0.6 convolution_convert_fusion.4
  67.3 0.2 copy.37
  67.5 0.7 copy-done.8
  68.2 0.1 copy.49
  68.4 0.9 multiply_reduce_fusion.1
  69.3 0.1 convert_element_type.193
  69.4 0.9 multiply_cosine_fusion
  70.3 0.1 subtract_convert_fusion
  70.5 0.1 maximum_bitcast_fusion
  70.6 1.5 convolution_convert_fusion.3
  72.1 0.1 maximum_maximum_fusion
  72.3 0.5 slice.46
  72.8 0.1 select_reduce_fusion.inv_ref
  72.9 4.0 %copy-done.2 = bf16[2,4,4,2,128,640]{5,4,3,2,1,0:T(8,128)(2,1)S(1)} copy-done((bf16[2,4,4,2,128,640]{5,4,3,2,1,0:T(8,128)(2,1)S(1)}, bf16[2,4,4,2,128,640]{5,4,3,2,1,0:T(8,128)(2,1)}, u32[]{:S(2)}) %copy-start.2) | copy-done | bytes 10485784
  76.9 27.9 %attention.1 = bf16[2,256,512]{2,1,0:T(8,128)(2,1)S(1)} custom-call(s32[64]{0:T(128)S(1)} %select_reduce_fusion.inv_ref, s32[1]{0:T(128)} %bitcast.1.blk_ref, bf16[2,256,640]{2,1,0:T(8,128)(2,1)S(1)} %bitcast.93, bf16[64,128,640]{2,1,0:T(8,128)(2,1)S(1)} %bitcast.90), custom_call_target="tpu_custom_call" | custom-call | tf_op jit(solution)/shard_map/attention/pallas_call | solution.py:275
  104.9 0.3 convolution_convert_fusion.5
  105.2 1.2 copy-done.6
  106.4 0.5 convolution_convert_fusion
  106.9 13.9 %tp_scatter.1 = bf16[4,32,2048]{2,1,0:T(8,128)(2,1)S(1)} custom-call(bf16[4,32,2048]{2,1,0:T(8,128)(2,1)S(1)} %bitcast.95), custom_call_target="tpu_custom_call" | custom-call | tf_op jit(solution)/shard_map/tp_scatter/pallas_call | solution.py:338
  120.8 0.1 convert_reduce_fusion.1
  120.9 0.2 fusion.12
  121.1 0.1 fusion.14.p_ref
  121.2 30.8 %column_gather.1 = bf16[8,32,2048]{2,1,0:T(8,128)(2,1)S(1)} custom-call(bf16[32,2048]{1,0:T(8,128)(2,1)S(1)} %fusion.14.p_ref), custom_call_target="tpu_custom_call" | custom-call | tf_op jit(solution)/shard_map/column_gather/pallas_call | solution.py:338
  152.0 1.0 copy-done.3
  153.0 0.1 iota.157
  153.2 0.1 iota.160
  153.4 0.1 iota.163
  153.5 0.1 compare_reduce_fusion
  153.6 0.3 fusion.3
  154.0 0.2 bitcast_compare_fusion
  154.2 3.1 convolution_convert_fusion.1
  157.3 0.1 iota.178
  157.4 0.2 bitcast_compare_fusion.1
  157.7 3.1 convolution_convert_fusion.2
  160.8 2.6 copy.45
  163.4 2.6 copy.46
  165.9 116.7 %experts.1 = (bf16[4,256,1024]{2,1,0:T(8,128)(2,1)}, bf16[4,256,1024]{2,1,0:T(8,128)(2,1)}) custom-call(bf16[4,256,1024]{2,1,0:T(8,128)(2,1)} %bitcast.102, bf16[4,256,1024]{2,1,0:T(8,128)(2,1)} %bitcast.101, bf16[2048,352]{1,0:T(8,128)(2,1)} %bitcast.103, bf16[2048,352]{1,0:T(8,128)(2,1)} %bitcast.104, bf16[352,2048]{1,0:T(8,128)(2,1)} %bitcast.113), custom_call_target="tpu_custom_call" | custom-call | tf_op jit(solution)/shard_map/experts/pallas_call | solution.py:503
  282.6 0.1 fusion.18
  282.7 0.2 select_convert_fusion.1
  283.0 2.5 fusion.44
  285.4 0.2 fusion.4
  285.7 0.7 fusion
  286.4 0.3 select_convert_fusion
  286.7 0.6 copy-done.4
  287.3 0.7 fusion.45
  288.0 0.2 fusion.5
  288.2 0.7 fusion.1
  288.9 0.1 pad_maximum_fusion.p_ref
  289.0 27.6 %column_scatter.1 = bf16[8,32,2048]{2,1,0:T(8,128)(2,1)S(1)} custom-call(bf16[8,32,2048]{2,1,0:T(8,128)(2,1)S(1)} %pad_maximum_fusion.p_ref), custom_call_target="tpu_custom_call" | custom-call | tf_op jit(solution)/shard_map/column_scatter/pallas_call | solution.py:338
  316.6 0.1 convert_reduce_fusion
  316.7 0.7 fusion.15
  (58 shorter events, 0.6 us)
Async XLA Ops:
  0.0 66.7 %copy-start = (bf16[2048,768]{1,0:T(8,128)(2,1)S(1)}, bf16[2048,768]{1,0:T(8,128)(2,1)}, u32[]{:S(2)}) copy-start(bf16[2048,768]{1,0:T(8,128)(2,1)} %param.18) | copy-start | bytes 9437188
  0.0 6.9 %copy-start.17 = (f32[512]{0:T(512)S(1)}, f32[512]{0:T(512)}, u32[]{:S(2)}) copy-start(f32[512]{0:T(512)} %param.20) | copy-start | bytes 6148
  0.0 7.4 %copy-start.14 = (s32[128,6]{0,1:T(8,128)S(1)}, s32[128,6]{0,1:T(8,128)}, u32[]{:S(2)}) copy-start(s32[128,6]{0,1:T(8,128)} %param.28) | copy-start | bytes 9220
  0.0 7.9 %copy-start.13 = (f32[128,6]{0,1:T(8,128)S(1)}, f32[128,6]{0,1:T(8,128)}, u32[]{:S(2)}) copy-start(f32[128,6]{0,1:T(8,128)} %param.29) | copy-start | bytes 9220
  6.7 0.5 copy-start.16
  7.3 0.6 copy-start.10
  62.7 4.0 %copy-start.1 = (bf16[2,4,4,2,128,640]{5,4,3,2,1,0:T(8,128)(2,1)}, bf16[2,4,4,2,128,640]{5,4,3,2,1,0:T(8,128)(2,1)S(1)}, u32[]{:S(2)}) copy-start(bf16[2,4,4,2,128,640]{5,4,3,2,1,0:T(8,128)(2,1)S(1)} %get-tuple-element.11) | copy-start | bytes 31457284
  67.5 0.7 copy-start.8
  68.4 3.7 %copy-start.11 = (bf16[640]{0:T(1024)(128)(2,1)S(1)}, bf16[640]{0:T(1024)(128)(2,1)}, u32[]{:S(2)}) copy-start(bf16[640]{0:T(1024)(128)(2,1)} %copy-done.10) | copy-start | bytes 3844
  70.5 2.3 copy-start.15
  72.9 4.0 %copy-start.2 = (bf16[2,4,4,2,128,640]{5,4,3,2,1,0:T(8,128)(2,1)S(1)}, bf16[2,4,4,2,128,640]{5,4,3,2,1,0:T(8,128)(2,1)}, u32[]{:S(2)}) copy-start(bf16[2,4,4,2,128,640]{5,4,3,2,1,0:T(8,128)(2,1)} %copy-done.1) | copy-start | bytes 31457284
  76.9 28.0 %copy-start.9 = (bf16[4,512,128]{2,1,0:T(8,128)(2,1)S(1)}, bf16[4,512,128]{2,1,0:T(8,128)(2,1)}, u32[]{:S(2)}) copy-start(bf16[4,512,128]{2,1,0:T(8,128)(2,1)} %param.22) | copy-start | bytes 1572868
  104.8 1.6 copy-start.6
  106.4 14.5 %copy-start.7 = (bf16[32,2048]{1,0:T(8,128)(2,1)S(1)}, bf16[32,2048]{1,0:T(8,128)(2,1)}, u32[]{:S(2)}) copy-start(bf16[32,2048]{1,0:T(8,128)(2,1)} %param.15) | copy-start | bytes 393220
  106.4 14.6 %copy-start.12 = (f32[2048]{0:T(1024)S(1)}, f32[2048]{0:T(1024)}, u32[]{:S(2)}) copy-start(f32[2048]{0:T(1024)} %param.24) | copy-start | bytes 24580
  152.0 1.0 copy-start.3
  283.0 2.7 copy-start.5
  285.7 1.6 copy-start.4

commit v2 on v1

v2 whole, which is shorter than its diff:
```python
import functools
import math

import jax
import jax.numpy as jnp
from jax import lax
from jax.experimental import pallas as pl
from jax.experimental.pallas import tpu as pltpu
from jax.sharding import PartitionSpec as P

EPSILON = 1e-06
MESH = pl.DeviceIdType.MESH
BF = jnp.bfloat16
F32 = jnp.float32
KEYW = 640


def place():
    s = lax.axis_index("seq")
    t = lax.axis_index("tp")
    return (s // 32) * 4 + t, (s // 8) % 4, (s // 2) % 4, s % 2


def dev(z, y, x, c):
    z, y, x, c = z % 8, y % 4, x % 4, c % 2
    return ((z // 4) * 32 + y * 8 + x * 2 + c, z % 4)


def greet(peers):
    barrier = pltpu.get_barrier_semaphore()
    for p in peers:
        pl.semaphore_signal(barrier, inc=1, device_id=p, device_id_type=MESH)
    pl.semaphore_wait(barrier, len(peers))


def rcopy(src, dst, ss, rs, device):
    return pltpu.make_async_remote_copy(
        src_ref=src, dst_ref=dst, send_sem=ss, recv_sem=rs, device_id=device, device_id_type=MESH
    )


def normalize(values, gain_vec):
    values = values.astype(F32)
    factor = lax.rsqrt(jnp.mean(values * values, axis=-1, keepdims=True) + EPSILON)
    return values * factor * gain_vec


def rotate(values, position):
    half_width = values.shape[-1] // 2
    frequency = jnp.exp(
        jnp.arange(half_width, dtype=F32) * (-2.0 * math.log(10000.0) / values.shape[-1])
    )
    angles = position.astype(F32).reshape(position.shape + (1,) * (values.ndim - 1)) * frequency
    cosine = jnp.cos(angles)
    sine_part = jnp.sin(angles)
    first_half = values[..., :half_width]
    second_half = values[..., half_width:]
    return jnp.concatenate(
        [
            first_half * cosine - second_half * sine_part,
            second_half * cosine + first_half * sine_part,
        ],
        axis=-1,
    )


def gather_kernel(kv_ref, nt_ref, rg_ref, KV, NT, RG, ssem, rsem, lsem):
    z, y, x, c = place()
    zh, t = z // 4, z % 4
    peers = [dev(z + k, y, x, c) for k in range(1, 8)]
    xs = [dev(z, y, x + 1, c), dev(z, y, x + 3, c), dev(z, y, x + 2, c)]
    ys = [dev(z, y + 1, x, c), dev(z, y + 3, x, c), dev(z, y + 2, x, c)]
    other = dev(z, y, x, c + 1)
    greet(peers + xs + ys + [other])
    number = [0]
    sent = []

    def send(src, dst, device):
        i = number[0]
        number[0] += 1
        cp = rcopy(src, dst, ssem.at[i], rsem.at[i], device)
        cp.start()
        sent.append(cp)
        return i

    def arrived(i, region):
        rcopy(region, region, ssem.at[i], rsem.at[i], other).wait_recv()

    rows = pl.ds(pl.multiple_of(t * 32, 32), 32)
    zi = {}
    mine = KV.at[zh, y, x, c, rows]
    for k in (4, 3, 5, 2, 6, 1, 7):
        zi[k] = send(kv_ref, mine, dev(z + k, y, x, c))
    locals_ = [
        pltpu.make_async_copy(kv_ref, mine, lsem.at[0]),
        pltpu.make_async_copy(nt_ref, NT.at[t], lsem.at[1]),
        pltpu.make_async_copy(rg_ref, RG.at[0, 0, zh], lsem.at[2]),
    ]
    for cp in locals_:
        cp.start()
    ri = send(rg_ref, RG.at[0, 0, zh], dev(z + 4, y, x, c))
    ti = {}
    for k in (3, 2, 1):
        ti[k] = send(nt_ref, NT.at[t], (zh * 32 + y * 8 + x * 2 + c, (t + k) % 4))
    for cp in locals_:
        cp.wait()
    for k in zi:
        zz = (z - k + 8) % 8
        arrived(zi[k], KV.at[zz // 4, y, x, c, pl.ds(pl.multiple_of((zz % 4) * 32, 32), 32)])
    arrived(ri, RG.at[0, 0, 1 - zh])
    spare = pltpu.make_async_copy(RG.at[0, 0], RG.at[1, 0], lsem.at[2])
    spare.start()
    routes_sent = []
    for k in (1, 2, 3):
        g = RG.at[0, 0]
        routes_sent.append((send(g, RG.at[0, k], dev(z, y, x + k, c)), RG.at[0, k]))
        routes_sent.append((send(g, RG.at[1, k], dev(z, y + k, x, c)), RG.at[1, k]))
    lo, hi = pl.ds(0, 64), pl.ds(64, 64)
    xm, xp, xo = (x + 3) % 4, (x + 1) % 4, (x + 2) % 4
    ym, yp, yo = (y + 3) % 4, (y + 1) % 4, (y + 2) % 4
    a, b = KV.at[0, y, x, c], KV.at[1, y, x, c]
    ap = send(a, a, xs[0])
    am = send(a, a, xs[1])
    bp = send(b, b, ys[0])
    bm = send(b, b, ys[1])
    arrived(ap, KV.at[0, y, xm, c])
    g = KV.at[0, y, xm, c, lo]
    ap2 = send(g, g, xs[0])
    arrived(bp, KV.at[1, ym, x, c])
    g = KV.at[1, ym, x, c, lo]
    bp2 = send(g, g, ys[0])
    arrived(am, KV.at[0, y, xp, c])
    g = KV.at[0, y, xp, c, hi]
    am2 = send(g, g, xs[1])
    arrived(bm, KV.at[1, yp, x, c])
    g = KV.at[1, yp, x, c, hi]
    bm2 = send(g, g, ys[1])
    arrived(ap2, KV.at[0, y, xo, c, lo])
    arrived(am2, KV.at[0, y, xo, c, hi])
    r = KV.at[0, y, :, c]
    rp = send(r, r, ys[0])
    rm = send(r, r, ys[1])
    arrived(bp2, KV.at[1, yo, x, c, lo])
    arrived(bm2, KV.at[1, yo, x, c, hi])
    q = KV.at[1, :, x, c]
    qp = send(q, q, xs[0])
    qm = send(q, q, xs[1])
    across = [send(r, r, other), send(q, q, other)]
    arrived(rp, KV.at[0, ym, :, c])
    g = KV.at[0, ym, :, c, lo]
    rp2 = send(g, g, ys[0])
    arrived(qp, KV.at[1, :, xm, c])
    g = KV.at[1, :, xm, c, lo]
    qp2 = send(g, g, xs[0])
    arrived(rm, KV.at[0, yp, :, c])
    g = KV.at[0, yp, :, c, hi]
    rm2 = send(g, g, ys[1])
    arrived(qm, KV.at[1, :, xp, c])
    g = KV.at[1, :, xp, c, hi]
    qm2 = send(g, g, xs[1])
    for g in (KV.at[0, ym, :, c], KV.at[1, :, xm, c], KV.at[0, yp, :, c], KV.at[1, :, xp, c]):
        across.append(send(g, g, other))
    arrived(rp2, KV.at[0, yo, :, c, lo])
    arrived(rm2, KV.at[0, yo, :, c, hi])
    g = KV.at[0, yo, :, c]
    across.append(send(g, g, other))
    arrived(qp2, KV.at[1, :, xo, c, lo])
    arrived(qm2, KV.at[1, :, xo, c, hi])
    g = KV.at[1, :, xo, c]
    across.append(send(g, g, other))
    d = 1 - c
    for i, region in zip(
        across,
        (
            KV.at[0, y, :, d],
            KV.at[1, :, x, d],
            KV.at[0, ym, :, d],
            KV.at[1, :, xm, d],
            KV.at[0, yp, :, d],
            KV.at[1, :, xp, d],
            KV.at[0, yo, :, d],
            KV.at[1, :, xo, d],
        ),
    ):
        arrived(i, region)
    for k in ti:
        arrived(ti[k], NT.at[(t - k + 4) % 4])
    spare.wait()
    for i, region in routes_sent:
        arrived(i, region)
    for cp in sent:
        cp.wait_send()


def gather_keys(kv_own, normed_own, rg):
    count = 48
    vm = pl.BlockSpec(memory_space=pltpu.VMEM)
    return pl.pallas_call(
        gather_kernel,
        out_shape=(
            jax.ShapeDtypeStruct((2, 4, 4, 2, 128, KEYW), BF),
            jax.ShapeDtypeStruct((4, 32, 2048), BF),
            jax.ShapeDtypeStruct((2, 4, 2, 16, 128), F32),
        ),
        in_specs=[vm, vm, vm],
        out_specs=(pl.BlockSpec(memory_space=pltpu.HBM), vm, vm),
        scratch_shapes=[
            pltpu.SemaphoreType.DMA((count,)),
            pltpu.SemaphoreType.DMA((count,)),
            pltpu.SemaphoreType.DMA((3,)),
        ],
        compiler_params=pltpu.CompilerParams(
            collective_id=0, has_side_effects=True, vmem_limit_bytes=16 * 2**20
        ),
        name="gather_keys",
    )(kv_own, normed_own, rg)


CHUNK = 1024


def attention_kernel(inv_ref, blk_ref, q_ref, kv_hbm, o_ref, kbuf, m_ref, l_ref, acc_ref, sems):
    low = blk_ref[0]
    per = CHUNK // 64
    top_chunks = (127 - low) // per + 1

    def issue(p, carry):
        second = p >= 64
        d = inv_ref[jnp.where(second, 127 - p, p)]
        off = pl.multiple_of(jnp.where(second, 64, 0), 64)
        pltpu.make_async_copy(
            kv_hbm.at[d, pl.ds(off, 64)],
            kbuf.at[pl.ds(pl.multiple_of(p * 64, 64), 64)],
            sems.at[p // per],
        ).start()
        return carry

    lax.fori_loop(0, top_chunks * per, issue, 0)
    scale = (128 + 64) ** (-0.5)

    for half in (1, 0):
        block = low if half == 0 else 127 - low
        last = block // per
        m_ref[...] = jnp.full_like(m_ref, -1e30)
        l_ref[...] = jnp.zeros_like(l_ref)
        acc_ref[...] = jnp.zeros_like(acc_ref)

        def step(ch, masked):
            region = kbuf.at[pl.ds(pl.multiple_of(ch * CHUNK, CHUNK), CHUNK)]
            if half == 1:
                pltpu.make_async_copy(region, region, sems.at[ch]).wait()
            keys = region[...]
            s = jnp.dot(keys, q_ref[half], preferred_element_type=F32) * scale
            if masked:
                key = lax.broadcasted_iota(jnp.int32, s.shape, 0)
                query = lax.broadcasted_iota(jnp.int32, s.shape, 1) % 64
                s = jnp.where(key - query <= block * 64 - ch * CHUNK, s, -1e30)
            m_old = m_ref[...]
            m_new = jnp.maximum(m_old, jnp.max(s, axis=0, keepdims=True))
            p = jnp.exp(s - m_new)
            alpha = jnp.exp(m_old - m_new)
            l_ref[...] = l_ref[...] * alpha + jnp.sum(p, axis=0, keepdims=True)
            m_ref[...] = m_new
            acc_ref[...] = acc_ref[...] * alpha + lax.dot_general(
                keys[:, :512], p.astype(BF), (((0,), (0,)), ((), ())), preferred_element_type=F32
            )

        def loop(ch, carry):
            step(ch, False)
            return carry

        lax.fori_loop(0, last, loop, 0)
        step(last, True)
        o_ref[half] = (acc_ref[...] / l_ref[...]).T.astype(BF)


def attention(inv, low, q, kv):
    return pl.pallas_call(
        attention_kernel,
        out_shape=jax.ShapeDtypeStruct((2, 256, 512), BF),
        in_specs=[
            pl.BlockSpec(memory_space=pltpu.SMEM),
            pl.BlockSpec(memory_space=pltpu.SMEM),
            pl.BlockSpec(memory_space=pltpu.VMEM),
            pl.BlockSpec(memory_space=pltpu.HBM),
        ],
        out_specs=pl.BlockSpec(memory_space=pltpu.VMEM),
        scratch_shapes=[
            pltpu.VMEM((8192, KEYW), BF),
            pltpu.VMEM((1, 256), F32),
            pltpu.VMEM((1, 256), F32),
            pltpu.VMEM((512, 256), F32),
            pltpu.SemaphoreType.DMA((8192 // CHUNK,)),
        ],
        compiler_params=pltpu.CompilerParams(vmem_limit_bytes=32 * 2**20),
        name="attention",
    )(inv, low, q, kv)


def tp_scatter_kernel(p_ref, o_ref, ssem, rsem, lsem):
    z, y, x, c = place()
    s, t = lax.axis_index("seq"), lax.axis_index("tp")
    greet([(s, (t + k) % 4) for k in (1, 2, 3)])
    cps = []
    for k in (2, 3, 1):
        to = (t + k) % 4
        cp = rcopy(p_ref.at[to], o_ref.at[k], ssem.at[k], rsem.at[k], (s, to))
        cp.start()
        cps.append(cp)
    own = pltpu.make_async_copy(p_ref.at[t], o_ref.at[0], lsem)
    own.start()
    own.wait()
    for cp in cps:
        cp.wait()


def column_gather_kernel(p_ref, o_ref, ssem, rsem, lsem):
    z, y, x, c = place()
    towards = (dev(z + 1, y, x, c), dev(z + 7, y, x, c))
    greet(towards)

    def shard(d, s):
        return (z + 8 - s) % 8 if d == 0 else (z + s) % 8

    def hop(d, s, h):
        rows = pl.ds(h * 16, 16)
        src = p_ref.at[rows] if s == 1 else o_ref.at[shard(d, s - 1), rows]
        return rcopy(
            src, o_ref.at[shard(d, s - 1), rows], ssem.at[d, s - 1, h], rsem.at[d, s - 1, h],
            towards[d],
        )

    def arrived(d, s, h):
        region = o_ref.at[shard(d, s), pl.ds(h * 16, 16)]
        rcopy(region, region, ssem.at[d, s - 1, h], rsem.at[d, s - 1, h], towards[d]).wait_recv()

    for h in (0, 1):
        for d in (0, 1):
            hop(d, 1, h).start()
    own = pltpu.make_async_copy(p_ref, o_ref.at[z], lsem)
    own.start()
    for s in (2, 3, 4):
        for h in (0, 1):
            for d in (0, 1):
                arrived(d, s - 1, h)
                if s < 4 or h == d:
                    hop(d, s, h).start()
    own.wait()
    for d in (0, 1):
        arrived(d, 4, d)
        for s in (1, 2, 3):
            for h in (0, 1):
                hop(d, s, h).wait_send()
        hop(d, 4, d).wait_send()


def column_gather(array):
    vm = pl.BlockSpec(memory_space=pltpu.VMEM)
    return pl.pallas_call(
        column_gather_kernel,
        out_shape=jax.ShapeDtypeStruct((8, 32, 2048), BF),
        in_specs=[vm],
        out_specs=vm,
        scratch_shapes=[
            pltpu.SemaphoreType.DMA((2, 4, 2)),
            pltpu.SemaphoreType.DMA((2, 4, 2)),
            pltpu.SemaphoreType.DMA,
        ],
        compiler_params=pltpu.CompilerParams(
            collective_id=2, has_side_effects=True, vmem_limit_bytes=16 * 2**20
        ),
        name="column_gather",
    )(array)


def column_scatter_kernel(p_ref, o_ref, rbuf, sbuf, ssem, rsem):
    z, y, x, c = place()
    towards = (dev(z + 1, y, x, c), dev(z + 7, y, x, c))
    greet(towards)

    def target(d, s):
        return (z + 5 - s) % 8 if d == 0 else (z + 3 + s) % 8

    def hop(d, s, h, src):
        rows = pl.ds(h * 16, 16)
        return rcopy(
            src.at[rows], rbuf.at[d, s - 1, rows], ssem.at[d, s - 1, h], rsem.at[d, s - 1, h],
            towards[d],
        )

    started = []
    for d in (0, 1):
        cp = hop(d, 1, d, p_ref.at[target(d, 1)])
        cp.start()
        started.append(cp)
    for d in (0, 1):
        cp = hop(d, 2, 1 - d, p_ref.at[target(d, 2)])
        cp.start()
        started.append(cp)
    for s in (2, 3, 4):
        for h in (0, 1):
            todo = []
            for d in (0, 1):
                if s == 2 and h != d:
                    continue
                rows = pl.ds(h * 16, 16)
                hop(d, s - 1, h, sbuf.at[d, s - 1]).wait_recv()
                sbuf[d, s - 1, rows] = (
                    p_ref[target(d, s), rows].astype(F32) + rbuf[d, s - 2, rows].astype(F32)
                ).astype(BF)
                todo.append(hop(d, s, h, sbuf.at[d, s - 1]))
            for cp in todo:
                cp.start()
                started.append(cp)
    for h in (0, 1):
        for d in (0, 1):
            hop(d, 4, h, sbuf.at[d, 3]).wait_recv()
    o_ref[...] = (
        p_ref[z].astype(F32) + rbuf[0, 3].astype(F32) + rbuf[1, 3].astype(F32)
    )
    for cp in started:
        cp.wait_send()


def column_scatter(array):
    vm = pl.BlockSpec(memory_space=pltpu.VMEM)
    return pl.pallas_call(
        column_scatter_kernel,
        out_shape=jax.ShapeDtypeStruct((32, 2048), F32),
        in_specs=[vm],
        out_specs=vm,
        scratch_shapes=[
            pltpu.VMEM((2, 4, 32, 2048), BF),
            pltpu.VMEM((2, 4, 32, 2048), BF),
            pltpu.SemaphoreType.DMA((2, 4, 2)),
            pltpu.SemaphoreType.DMA((2, 4, 2)),
        ],
        compiler_params=pltpu.CompilerParams(
            collective_id=3, has_side_effects=True, vmem_limit_bytes=16 * 2**20
        ),
        name="column_scatter",
    )(array)


def exchange(kernel, name, cid, array, out):
    vm = pl.BlockSpec(memory_space=pltpu.VMEM)
    return pl.pallas_call(
        kernel,
        out_shape=jax.ShapeDtypeStruct(out, BF),
        in_specs=[vm],
        out_specs=vm,
        scratch_shapes=[
            pltpu.SemaphoreType.DMA((8,)),
            pltpu.SemaphoreType.DMA((8,)),
            pltpu.SemaphoreType.DMA,
        ],
        compiler_params=pltpu.CompilerParams(
            collective_id=cid, has_side_effects=True, vmem_limit_bytes=16 * 2**20
        ),
        name=name,
    )(array)


def turn(i):
    return ((i * (i + 1)) // 2) % 4


def experts_kernel(
    xin, sla, slb, gta, gtb, wg, wu, wd, out,
    ta, tb, sa, sb, ra, rb, oa, ob, ma, mb, pa, pb, qa, qb,
    s1, r1, s2a, r2a, s2b, r2b, s3a, r3a, s3b, r3b, s4, r4, lsem,
):
    z, y, x, c = place()
    peers = [dev(z, y, x, c + 1)]
    for k in (1, 2, 3):
        for d in (0, 1):
            peers.append(dev(z, y + k, x, c + d))
            peers.append(dev(z, y, x + k, c + d))
    greet(peers)
    left, right = pl.ds(0, 1024), pl.ds(1024, 1024)
    low, high = pl.ds(0, 128), pl.ds(128, 128)

    def blk(j):
        return pl.ds(pl.multiple_of(j * 32, 32), 32)

    def where_x(k):
        return dev(z, y, x + k, c)

    def where_y(k):
        return dev(z, y + k, x, c)

    def first(k):
        return (
            rcopy(xin.at[:, left], ta.at[k], s1.at[0, k], r1.at[0, k], where_x(k)),
            rcopy(xin.at[:, right], tb.at[k], s1.at[1, k], r1.at[1, k], where_y(k)),
        )

    def onward(k):
        rows, i = (low, 2) if k == 1 else (high, 0)
        return (
            rcopy(ta.at[k, rows], ta.at[2, rows], s1.at[0, i], r1.at[0, i], where_x(k)),
            rcopy(tb.at[k, rows], tb.at[2, rows], s1.at[1, i], r1.at[1, i], where_y(k)),
        )

    for k in (1, 3):
        for cp in first(k):
            cp.start()
    ta[0] = xin[:, :1024]
    tb[0] = xin[:, 1024:]

    def hop2a(k, j):
        return rcopy(
            sa.at[k, blk(j)], ra.at[k, blk(j)], s2a.at[k, j], r2a.at[k, j],
            dev(z, y + j // 2, x, c + j % 2),
        )

    def hop2b(k, j):
        return rcopy(
            sb.at[k, blk(j)], rb.at[j // 2, blk(k * 2 + j % 2)], s2b.at[k, j], r2b.at[k, j],
            dev(z, y, x + j // 2, c + j % 2),
        )

    def own2(k):
        return (
            pltpu.make_async_copy(sa.at[k, blk(0)], ra.at[k, blk(0)], lsem.at[k]),
            pltpu.make_async_copy(sb.at[k, blk(0)], rb.at[0, blk(k * 2)], lsem.at[4 + k]),
        )

    number = lax.broadcasted_iota(jnp.int32, (8, 32, 256), 1).astype(F32)

    def table(slots, k):
        return (slots[k][:, None, :] == number).astype(F32)

    def spread(i, carry):
        k = turn(i)

        @pl.when(i == 1)
        def _():
            for n in (1, 3):
                for cp, cp2 in zip(first(n), onward(n)):
                    cp.wait_recv()
                    cp2.start()

        @pl.when(i == 3)
        def _():
            for n in (1, 3):
                for cp in onward(n):
                    cp.wait_recv()

        sa[k] = jnp.dot(
            table(sla, k).reshape(256, 256).astype(BF), ta[k], preferred_element_type=F32
        ).astype(BF)
        sb[k] = jnp.dot(
            table(slb, k).reshape(256, 256).astype(BF), tb[k], preferred_element_type=F32
        ).astype(BF)
        for j in (2, 6, 4, 3, 7, 5, 1):
            hop2a(k, j).start()
            hop2b(k, j).start()
        for cp in own2(k):
            cp.start()
        return carry

    lax.fori_loop(0, 4, spread, 0)

    def hop3a(k, j):
        return rcopy(
            oa.at[k, blk(j)], ma.at[k, blk(j)], s3a.at[k, j], r3a.at[k, j],
            dev(z, y + 4 - j // 2, x, c + j % 2),
        )

    def hop3b(k, j):
        return rcopy(
            ob.at[k, blk(j)], mb.at[j // 2, blk(k * 2 + j % 2)], s3b.at[k, j], r3b.at[k, j],
            dev(z, y, x + 4 - k, c + j % 2),
        )

    def own3(k):
        return (
            pltpu.make_async_copy(oa.at[k, blk(0)], ma.at[k, blk(0)], lsem.at[8 + k]),
            pltpu.make_async_copy(ob.at[0, blk(k * 2)], mb.at[k, blk(0)], lsem.at[12 + k]),
        )

    for k in range(4):
        for cp in own2(k):
            cp.wait()

    def across(rows, weight):
        return lax.dot_general(
            rows, weight, (((1,), (1,)), ((), ())), preferred_element_type=F32
        )

    def work(i, carry):
        k = turn(i)
        for j in range(1, 8):
            hop2a(k, j).wait_recv()
        for n in range(4):
            hop2b(n, k * 2 + 1).wait_recv()

        @pl.when(i > 0)
        def _():
            for n in range(4):
                hop2b(n, k * 2).wait_recv()

        rows_a = ra[k]
        rows_b = rb[k]
        gate = across(rows_a, wg[:, :1024]) + across(rows_b, wg[:, 1024:])
        up = across(rows_a, wu[:, :1024]) + across(rows_b, wu[:, 1024:])
        hidden = (gate / (1.0 + jnp.exp(-gate)) * up).astype(BF)
        oa[k] = jnp.dot(hidden, wd[:, :1024], preferred_element_type=F32).astype(BF)
        ob[k] = jnp.dot(hidden, wd[:, 1024:], preferred_element_type=F32).astype(BF)
        for j in range(1, 8):
            hop3a(k, j).start()
        own3(k)[0].start()

        @pl.when(i > 0)
        def _():
            for j in (0, 2, 4, 6):
                hop3b(k, j).start()

        for j in (1, 3, 5, 7):
            hop3b(k, j).start()
        return carry

    def work_first():
        for j in range(4):
            own3(j)[1].start()

    lax.fori_loop(0, 1, work, 0)
    work_first()
    lax.fori_loop(1, 4, work, 0)

    def back(k, side):
        if side == 0:
            return rcopy(pa.at[k], qa.at[k], s4.at[0, k], r4.at[0, k], where_x(4 - k))
        return rcopy(pb.at[k], qb.at[k], s4.at[1, k], r4.at[1, k], where_y(4 - k))

    def weigh(slots, gates, k, rows):
        w = table(slots, k) * gates[k][:, None, :]
        w = w.reshape(256, 256)
        hi = w.astype(BF)
        lo = (w - hi.astype(F32)).astype(BF)
        dims = (((0,), (0,)), ((), ()))
        return lax.dot_general(hi, rows, dims, preferred_element_type=F32) + lax.dot_general(
            lo, rows, dims, preferred_element_type=F32
        )

    def home_a(i, carry):
        k = turn(i)
        for j in range(1, 8):
            hop3a(k, j).wait_recv()
        own3(k)[0].wait()
        pa[k] = weigh(sla, gta, k, ma[k]).astype(BF)
        back(k, 0).start()
        return carry

    def home_b(i, carry):
        k = turn(i)
        for n in range(4):
            hop3b(n, k * 2 + 1).wait_recv()
            if n:
                hop3b(n, k * 2).wait_recv()
        own3(k)[1].wait()
        pb[k] = weigh(slb, gtb, k, mb[k]).astype(BF)
        back(k, 1).start()
        return carry

    lax.fori_loop(1, 4, home_a, 0)
    lax.fori_loop(1, 4, home_b, 0)
    for j in range(1, 8):
        hop3a(0, j).wait_recv()
    own3(0)[0].wait()
    for n in range(4):
        hop3b(n, 1).wait_recv()
        if n:
            hop3b(n, 0).wait_recv()
    own3(0)[1].wait()
    total_a = weigh(sla, gta, 0, ma[0])
    total_b = weigh(slb, gtb, 0, mb[0])
    for k in (1, 3, 2):
        back(k, 0).wait_recv()
        back(k, 1).wait_recv()
        total_a += qa[k].astype(F32)
        total_b += qb[k].astype(F32)
    out[:, :1024] = total_a.astype(BF)
    out[:, 1024:] = total_b.astype(BF)

    for k in (1, 3):
        for cp in first(k) + onward(k):
            cp.wait_send()
    for k in (1, 2, 3):
        back(k, 0).wait_send()
        back(k, 1).wait_send()

    def drain(k, carry):
        for j in range(1, 8):
            hop2a(k, j).wait_send()
            hop2b(k, j).wait_send()
            hop3a(k, j).wait_send()
        for j in (1, 3, 5, 7):
            hop3b(k, j).wait_send()

        @pl.when(k > 0)
        def _():
            for j in (0, 2, 4, 6):
                hop3b(k, j).wait_send()

        return carry

    lax.fori_loop(0, 4, drain, 0)


def experts(column, slots, gates, wg, wu, wd):
    vm = pl.BlockSpec(memory_space=pltpu.VMEM)
    big = (4, 256, 1024)
    dma = pltpu.SemaphoreType.DMA
    return pl.pallas_call(
        experts_kernel,
        out_shape=jax.ShapeDtypeStruct((256, 2048), BF),
        in_specs=[vm] * 8,
        out_specs=vm,
        scratch_shapes=[pltpu.VMEM(big, BF)] * 14
        + [
            dma((2, 4)), dma((2, 4)),
            dma((4, 8)), dma((4, 8)), dma((4, 8)), dma((4, 8)),
            dma((4, 8)), dma((4, 8)), dma((4, 8)), dma((4, 8)),
            dma((2, 4)), dma((2, 4)),
            dma((16,)),
        ],
        compiler_params=pltpu.CompilerParams(
            collective_id=4, has_side_effects=True, vmem_limit_bytes=60 * 2**20
        ),
        name="experts",
    )(column, slots[0], slots[1], gates[0], gates[1], wg, wu, wd)


def slot_tables(rgs, z, y, x, c):
    routes = rgs[:, :, :, :6].transpose(0, 1, 3, 2, 4).reshape(2, 4, 6, 256).astype(jnp.int32)
    gates = rgs[:, :, :, 8:14].transpose(0, 1, 3, 2, 4).reshape(2, 4, 6, 256)
    off = jnp.arange(8, dtype=jnp.int32) // 2
    core = (c + jnp.arange(8, dtype=jnp.int32) % 2) % 2
    base = (z // 4) * 32
    expert = jnp.stack(
        [base + ((y + off) % 4) * 8 + x * 2 + core, base + y * 8 + ((x + off) % 4) * 2 + core]
    )
    hit = routes[:, :, None] == expert[:, None, :, None, None]
    member = jnp.any(hit, axis=3)
    gate = jnp.sum(jnp.where(hit, gates[:, :, None], 0.0), axis=3)
    ti = lax.broadcasted_iota(jnp.int32, (256, 256), 0)
    tj = lax.broadcasted_iota(jnp.int32, (256, 256), 1)
    before = ((ti < tj) & (tj // 32 == ti // 32)).astype(BF)
    rank = jnp.dot(
        member.astype(BF).reshape(64, 256), before, preferred_element_type=F32
    ).reshape(member.shape)
    token = lax.broadcasted_iota(jnp.int32, member.shape, 3)
    slot = jnp.where(member, (token // 32 * 4).astype(F32) + rank, -1.0)
    return slot, gate


def body(
    tokens, block_ids, attn_gain, q_weight, kv_weight, kv_gain, uk_weight, uv_weight,
    o_weight, ffn_gain, w_gate, w_up, w_down, routes, gate_weights,
):
    z, y, x, c = place()
    t = lax.axis_index("tp")
    s = lax.axis_index("seq")
    own_blocks = lax.dynamic_slice(block_ids, (s, 0), (1, 2))[0]
    normed_own = normalize(tokens, attn_gain).astype(BF)
    own_pos = own_blocks[t // 2] * 64 + (t % 2) * 32 + jnp.arange(32, dtype=jnp.int32)
    projected = jnp.dot(normed_own, kv_weight, preferred_element_type=F32)
    latent = normalize(projected[:, :512], kv_gain).astype(BF)
    key_rope = rotate(projected[:, 512:], own_pos).astype(BF)
    kv_own = jnp.concatenate([latent, key_rope, jnp.zeros((32, 64), BF)], axis=1)
    pad2 = jnp.zeros((2, 128), F32)
    rg = jnp.concatenate([routes.astype(F32).T, pad2, gate_weights.T, pad2], axis=0)
    kv, normed, rgs = gather_keys(kv_own, normed_own, rg)

    normed = normed.reshape(128, 2048)
    query_pos = (own_blocks[:, None] * 64 + jnp.arange(64, dtype=jnp.int32)[None, :]).reshape(128)
    queries = jnp.dot(normed, q_weight, preferred_element_type=F32).astype(BF)
    queries = queries.reshape(128, 4, 192)
    query_rope = rotate(queries[..., 128:].astype(F32), query_pos).astype(BF)
    query_latent = jnp.einsum(
        "thn,hln->hlt", queries[..., :128], uk_weight, preferred_element_type=F32
    ).astype(BF)
    q = jnp.concatenate(
        [query_latent, query_rope.transpose(1, 2, 0), jnp.zeros((4, 64, 128), BF)], axis=1
    )
    q = q.reshape(4, KEYW, 2, 64).transpose(2, 1, 0, 3).reshape(2, KEYW, 256)
    ids = jnp.arange(64, dtype=jnp.int32)
    inv = jnp.sum(
        jnp.where(block_ids[:, 0][None, :] == ids[:, None], ids[None, :], 0), axis=1
    ).astype(jnp.int32)
    out_latent = attention(inv, own_blocks[:1], q, kv.reshape(64, 128, KEYW))
    out_latent = out_latent.reshape(2, 4, 64, 512).transpose(1, 0, 2, 3).reshape(4, 128, 512)
    head_out = jnp.einsum(
        "htl,hlv->thv", out_latent, uv_weight, preferred_element_type=F32
    ).astype(BF)
    partial_out = jnp.dot(head_out.reshape(128, 512), o_weight, preferred_element_type=F32)
    parts = exchange(
        tp_scatter_kernel, "tp_scatter", 1, partial_out.astype(BF).reshape(4, 32, 2048),
        (4, 32, 2048),
    )
    attn_own = jnp.sum(parts.astype(F32), axis=0)
    mixed = (tokens.astype(F32) + attn_own).astype(BF)
    normed_ffn = normalize(mixed, ffn_gain).astype(BF)
    column = column_gather(normed_ffn).reshape(256, 2048)
    slots, gates = slot_tables(rgs, z, y, x, c)
    combined = experts(column, slots, gates, w_gate[0].T, w_up[0].T, w_down[0])
    sums = column_scatter(combined.reshape(8, 32, 2048))
    return (mixed.astype(F32) + sums).astype(BF)


def solution(mesh):
    return jax.shard_map(
        body,
        mesh=mesh,
        in_specs=(
            P(("seq", "tp"), None), P(), P(), P(None, "tp"), P(), P(),
            P("tp", None, None), P("tp", None, None), P("tp", None), P(),
            P("seq", None, "tp"), P("seq", None, "tp"), P("seq", "tp", None),
            P("seq", None), P("seq", None),
        ),
        out_specs=P(("seq", "tp"), None),
        check_vma=False,
    )
```

time: 318 us -> 283 us (0.89)
  Pallas kernels: 272 us -> 239 us
  matrix products: 16.4 us -> 5.95 us
    pallas_call x3 -> x1, Pallas kernels: 72.3 us -> 13.6 us  [exchange(): pl.pallas_call(kernel, out_shape=jax.ShapeDtypeStruct(out, BF), in_specs=...]
    pallas_call x1 -> x3, Pallas kernels: 117 us -> 142 us  [the longest x1 106 us: experts(): pl.pallas_call(experts_kernel, out_shape=jax.ShapeDtypeStruct((256, 2048)...]
    dot_general x8 -> x2, matrix products: 12.6 us -> 1.42 us  [the longest x1 1.07 us: slot_tables(): jnp.dot(member.astype(BF).reshape(64, 256), before, preferred_element_typ...]
    unnamed x39 -> x25, local copies, waits for them, and re-layouts: 17.4 us -> 14 us
where the time goes in v2:
time: 283 us; the launch traced here: 279 us
  Pallas kernels  239 us (84%)
  local copies, waits for them, and re-layouts  22.9 us (8%)
  other arithmetic  10.5 us (4%)
  matrix products  5.95 us (2%)
    pallas_call x1, Pallas kernels, experts(): pl.pallas_call(experts_kernel, out_shape=jax.ShapeDtypeStruct((256, 2048)...  106 us
    pallas_call x1, Pallas kernels, gather_keys(): pl.pallas_call(gather_kernel, out_shape=(jax.ShapeDtypeStruct((2, 4, 4, 2...  57.7 us
    pallas_call x1, Pallas kernels, attention(): pl.pallas_call(attention_kernel, out_shape=jax.ShapeDtypeStruct((2, 256,...  25.3 us
    pallas_call x1, Pallas kernels, column_gather(): pl.pallas_call(column_gather_kernel, out_shape=jax.ShapeDtypeStruct((8, 3...  20.1 us
    pallas_call x1, Pallas kernels, column_scatter(): pl.pallas_call(column_scatter_kernel, out_shape=jax.ShapeDtypeStruct((32,...  16.6 us
    unnamed x25, local copies, waits for them, and re-layouts  14 us
    pallas_call x1, Pallas kernels, exchange(): pl.pallas_call(kernel, out_shape=jax.ShapeDtypeStruct(out, BF), in_specs=...  13.6 us

profile of v2, /device:TPU:1, one launch (start us, length us, event | category | flops | bytes accessed | tf_op | source)
XLA Modules:
  0.0 279.3 jit_solution(10696974950565778827)
XLA Ops:
  0.0 0.0 copy-start
  0.0 1.4 dynamic_slice.7
  2.1 1.0 fusion.3
  3.2 0.7 slice_bitcast_fusion.5
  3.9 0.1 select_reduce_fusion.inv_ref
  4.0 0.5 compare_and_fusion
  4.5 0.9 multiply_reduce_fusion.1
  5.4 0.5 slice.52
  5.9 0.1 add_convert_fusion.1
  6.0 0.1 convert_element_type.97
  6.1 0.1 pad.14.clone
  6.2 0.6 iota_shift-right-logical_fusion
  6.7 0.7 convert_bitcast_fusion.1
  7.4 0.7 pad_maximum_fusion.rg_ref
  8.1 1.0 fusion.5.nt_ref
  9.1 2.4 fusion.41
  11.6 0.1 multiply_reduce_fusion
  11.7 0.1 fusion.26
  11.9 0.0 copy-done.11
  11.9 0.1 multiply_convert_fusion
  12.0 0.1 maximum_maximum_fusion.1.kv_ref
  12.1 0.9 multiply_cosine_fusion
  13.0 57.7 %gather_keys.1 = (bf16[2,4,4,2,128,640]{5,4,3,2,1,0:T(8,128)(2,1)S(1)}, bf16[4,32,2048]{2,1,0:T(8,128)(2,1)S(1)}, f32[2,4,2,16,128]{4,3,2,1,0:T(8,128)S(1)}) custom-call(bf16[32,640]{1,0:T(8,128)(2,1)S(1)} %maximum_maximum_fusion.1.kv_ref, bf16[32,2048]{1,0:T(8,128)(2,1)S(1)} %fusion.5.nt_ref, f32[16,128]{1,0:T(8,128)S(1)} %pad_maximum_fusion.rg_ref), custom_call_target="tpu_custom_call" | custom-call | tf_op jit(solution)/shard_map/gather_keys/pallas_call | solution.py:198
  70.7 0.0 copy-start.1
  70.7 4.0 %copy-done.1 = bf16[2,4,4,2,128,640]{5,4,3,2,1,0:T(8,128)(2,1)} copy-done((bf16[2,4,4,2,128,640]{5,4,3,2,1,0:T(8,128)(2,1)}, bf16[2,4,4,2,128,640]{5,4,3,2,1,0:T(8,128)(2,1)S(1)}, u32[]{:S(2)}) %copy-start.1) | copy-done | bytes 10485784
  74.7 0.0 copy-done
  74.7 1.3 convolution_convert_fusion.2
  76.0 1.1 copy.28
  77.1 0.6 slice.71
  77.7 1.6 copy.38
  79.3 1.0 convert_element_type.95
  80.3 1.0 subtract_convert_fusion
  81.3 0.1 maximum_bitcast_fusion
  81.4 0.1 fusion.2
  81.5 0.1 compare_reduce_fusion
  81.7 0.6 slice_bitcast_fusion.1
  82.3 1.1 fusion.1
  83.3 0.6 slice_bitcast_fusion.3
  84.0 0.0 copy-done.8
  84.0 0.3 fusion
  84.3 0.1 maximum_maximum_fusion
  84.5 0.9 copy.31
  85.4 2.2 copy.32.q_ref
  87.5 4.0 %copy-done.2 = bf16[2,4,4,2,128,640]{5,4,3,2,1,0:T(8,128)(2,1)S(1)} copy-done((bf16[2,4,4,2,128,640]{5,4,3,2,1,0:T(8,128)(2,1)S(1)}, bf16[2,4,4,2,128,640]{5,4,3,2,1,0:T(8,128)(2,1)}, u32[]{:S(2)}) %copy-start.2) | copy-done | bytes 10485784
  91.5 1.1 copy-done.5
  92.6 25.3 %attention.1 = bf16[2,256,512]{2,1,0:T(8,128)(2,1)S(1)} custom-call(s32[64]{0:T(128)S(1)} %select_reduce_fusion.inv_ref, s32[1]{0:T(128)} %bitcast.1.blk_ref, bf16[2,640,256]{2,1,0:T(8,128)(2,1)S(1)} %copy-done.5, bf16[64,128,640]{2,1,0:T(8,128)(2,1)S(1)} %bitcast.66), custom_call_target="tpu_custom_call" | custom-call | tf_op jit(solution)/shard_map/attention/pallas_call | solution.py:278
  118.0 0.0 copy-start.6
  118.0 0.0 copy-done.9
  118.0 0.3 convolution_convert_fusion.3
  118.4 1.2 copy-done.6
  119.6 0.5 convolution_convert_fusion
  120.0 13.6 %tp_scatter.1 = bf16[4,32,2048]{2,1,0:T(8,128)(2,1)S(1)} custom-call(bf16[4,32,2048]{2,1,0:T(8,128)(2,1)S(1)} %bitcast.70), custom_call_target="tpu_custom_call" | custom-call | tf_op jit(solution)/shard_map/tp_scatter/pallas_call | solution.py:447
  133.6 0.1 convert_reduce_fusion
  133.7 0.0 copy-done.7
  133.7 0.2 fusion.7
  133.9 0.0 copy-done.10
  133.9 0.1 fusion.9.p_ref
  134.0 20.1 %column_gather.1 = bf16[8,32,2048]{2,1,0:T(8,128)(2,1)S(1)} custom-call(bf16[32,2048]{1,0:T(8,128)(2,1)S(1)} %fusion.9.p_ref), custom_call_target="tpu_custom_call" | custom-call | tf_op jit(solution)/shard_map/column_gather/pallas_call | solution.py:359
  154.1 0.0 copy-start.4
  154.1 1.0 copy-done.4
  155.1 105.7 %experts.1 = bf16[256,2048]{1,0:T(8,128)(2,1)} custom-call(bf16[256,2048]{1,0:T(8,128)(2,1)} %bitcast.68, f32[4,8,256]{2,1,0:T(8,128)} %get-tuple-element.24.sla, f32[4,8,256]{2,1,0:T(8,128)} %get-tuple-element.23.slb, f32[4,8,256]{2,1,0:T(8,128)} %get-tuple-element.22.gta, f32[4,8,256]{2,1,0:T(8,128)} %get-tuple-element.21.gtb, bf16[352,2048]{1,0:T(8,128)(2,1)} %bitcast.75, ...), custom_call_target="tpu_custom_call" | custom-call | tf_op jit(solution)/shard_map/experts/pallas_call | solution.py:716
  260.8 1.2 copy-done.3
  262.0 16.6 %column_scatter.1 = f32[32,2048]{1,0:T(8,128)S(1)} custom-call(bf16[8,32,2048]{2,1,0:T(8,128)(2,1)S(1)} %bitcast.67), custom_call_target="tpu_custom_call" | custom-call | tf_op jit(solution)/shard_map/column_scatter/pallas_call | solution.py:427
  278.7 0.7 fusion.10
  (19 shorter events, 0.1 us)
Async XLA Ops:
  0.0 74.7 %copy-start = (bf16[2048,768]{1,0:T(8,128)(2,1)S(1)}, bf16[2048,768]{1,0:T(8,128)(2,1)}, u32[]{:S(2)}) copy-start(bf16[2048,768]{1,0:T(8,128)(2,1)} %param.18) | copy-start | bytes 9437188
  0.0 11.9 %copy-start.11 = (f32[512]{0:T(512)S(1)}, f32[512]{0:T(512)}, u32[]{:S(2)}) copy-start(f32[512]{0:T(512)} %param.20) | copy-start | bytes 6148
  70.7 4.0 %copy-start.1 = (bf16[2,4,4,2,128,640]{5,4,3,2,1,0:T(8,128)(2,1)}, bf16[2,4,4,2,128,640]{5,4,3,2,1,0:T(8,128)(2,1)S(1)}, u32[]{:S(2)}) copy-start(bf16[2,4,4,2,128,640]{5,4,3,2,1,0:T(8,128)(2,1)S(1)} %get-tuple-element.9) | copy-start | bytes 31457284
  79.3 4.7 %copy-start.8 = (bf16[4,512,128]{2,1,0:T(8,128)(2,1)S(1)}, bf16[4,512,128]{2,1,0:T(8,128)(2,1)}, u32[]{:S(2)}) copy-start(bf16[4,512,128]{2,1,0:T(8,128)(2,1)} %param.21) | copy-start | bytes 1572868
  87.5 4.0 %copy-start.2 = (bf16[2,4,4,2,128,640]{5,4,3,2,1,0:T(8,128)(2,1)S(1)}, bf16[2,4,4,2,128,640]{5,4,3,2,1,0:T(8,128)(2,1)}, u32[]{:S(2)}) copy-start(bf16[2,4,4,2,128,640]{5,4,3,2,1,0:T(8,128)(2,1)} %copy-done.1) | copy-start | bytes 31457284
  91.5 1.1 copy-start.5
  92.6 25.4 %copy-start.9 = (bf16[4,512,128]{2,1,0:T(8,128)(2,1)S(1)}, bf16[4,512,128]{2,1,0:T(8,128)(2,1)}, u32[]{:S(2)}) copy-start(bf16[4,512,128]{2,1,0:T(8,128)(2,1)} %param.22) | copy-start | bytes 1572868
  118.0 1.6 copy-start.6
  119.6 14.1 %copy-start.7 = (bf16[32,2048]{1,0:T(8,128)(2,1)S(1)}, bf16[32,2048]{1,0:T(8,128)(2,1)}, u32[]{:S(2)}) copy-start(bf16[32,2048]{1,0:T(8,128)(2,1)} %param.15) | copy-start | bytes 393220
  119.6 14.3 %copy-start.10 = (f32[2048]{0:T(1024)S(1)}, f32[2048]{0:T(1024)}, u32[]{:S(2)}) copy-start(f32[2048]{0:T(1024)} %param.24) | copy-start | bytes 24580
  154.1 1.0 copy-start.4
  260.8 1.2 copy-start.3

commit v3 on v2

--- a/solution.py
+++ b/solution.py
@@ -210,7 +210,7 @@
             pltpu.SemaphoreType.DMA((3,)),
         ],
         compiler_params=pltpu.CompilerParams(
-            collective_id=0, has_side_effects=True, vmem_limit_bytes=16 * 2**20
+            collective_id=0, has_side_effects=True, vmem_limit_bytes=60 * 2**20
         ),
         name="gather_keys",
     )(kv_own, normed_own, rg)
@@ -292,7 +292,7 @@
             pltpu.VMEM((512, 256), F32),
             pltpu.SemaphoreType.DMA((8192 // CHUNK,)),
         ],
-        compiler_params=pltpu.CompilerParams(vmem_limit_bytes=32 * 2**20),
+        compiler_params=pltpu.CompilerParams(vmem_limit_bytes=60 * 2**20),
         name="attention",
     )(inv, low, q, kv)
 

time: 283 us -> 265 us (0.936)
  local copies, waits for them, and re-layouts: 22.9 us -> 11 us
  Pallas kernels: 239 us -> 232 us
    unnamed x25 -> x21, local copies, waits for them, and re-layouts: 14 us -> 2.51 us
    pallas_call x1, Pallas kernels: 25.3 us -> 18.7 us  [attention(): pl.pallas_call(attention_kernel, out_shape=jax.ShapeDtypeStruct((2, 256,...]
where the time goes in v3:
time: 265 us; the launch traced here: 261 us
  Pallas kernels  232 us (88%)
  other arithmetic  11.7 us (4%)
  local copies, waits for them, and re-layouts  11 us (4%)
  matrix products  6.3 us (2%)
    pallas_call x1, Pallas kernels, experts(): pl.pallas_call(experts_kernel, out_shape=jax.ShapeDtypeStruct((256, 2048)...  106 us
    pallas_call x1, Pallas kernels, gather_keys(): pl.pallas_call(gather_kernel, out_shape=(jax.ShapeDtypeStruct((2, 4, 4, 2...  60.4 us
    pallas_call x1, Pallas kernels, attention(): pl.pallas_call(attention_kernel, out_shape=jax.ShapeDtypeStruct((2, 256,...  18.7 us
    pallas_call x1, Pallas kernels, column_gather(): pl.pallas_call(column_gather_kernel, out_shape=jax.ShapeDtypeStruct((8, 3...  17.3 us
    pallas_call x1, Pallas kernels, column_scatter(): pl.pallas_call(column_scatter_kernel, out_shape=jax.ShapeDtypeStruct((32,...  15.6 us
    pallas_call x1, Pallas kernels, exchange(): pl.pallas_call(kernel, out_shape=jax.ShapeDtypeStruct(out, BF), in_specs=...  14 us

profile of v3, /device:TPU:1, one launch (start us, length us, event | category | flops | bytes accessed | tf_op | source)
XLA Modules:
  0.0 261.4 jit_solution(14123879717609434699)
XLA Ops:
  0.0 0.0 copy-start
  0.0 0.0 copy-start.9
  0.0 1.4 dynamic_slice.7
  2.1 1.0 fusion.3
  3.2 0.7 slice_bitcast_fusion.5
  3.9 0.7 select_reduce_fusion.inv_ref
  4.5 0.5 compare_and_fusion
  5.1 0.9 multiply_reduce_fusion.1
  5.9 0.5 slice.52
  6.4 0.1 add_convert_fusion.1
  6.5 0.1 convert_element_type.97
  6.6 0.1 pad.14.clone
  6.7 0.7 convert_bitcast_fusion.1
  7.4 1.3 pad_maximum_fusion.rg_ref
  8.7 1.0 fusion.5.nt_ref
  9.7 0.0 copy-start.5
  9.7 2.5 fusion.41
  12.2 0.1 multiply_reduce_fusion
  12.3 0.1 fusion.26
  12.5 0.0 copy-done.9
  12.5 0.1 multiply_convert_fusion
  12.5 0.7 maximum_maximum_fusion.1.kv_ref
  13.2 1.0 multiply_cosine_fusion
  14.2 0.0 copy-done.5
  14.2 60.4 %gather_keys.1 = (bf16[2,4,4,2,128,640]{5,4,3,2,1,0:T(8,128)(2,1)}, bf16[4,32,2048]{2,1,0:T(8,128)(2,1)}, f32[2,4,2,16,128]{4,3,2,1,0:T(8,128)}) custom-call(bf16[32,640]{1,0:T(8,128)(2,1)} %maximum_maximum_fusion.1.kv_ref, bf16[32,2048]{1,0:T(8,128)(2,1)} %copy-done.5, f32[16,128]{1,0:T(8,128)} %pad_maximum_fusion.rg_ref), custom_call_target="tpu_custom_call" | custom-call | tf_op jit(solution)/shard_map/gather_keys/pallas_call | solution.py:198
  74.6 0.0 copy-done
  74.6 1.6 convolution_convert_fusion.2
  76.2 0.2 copy.28
  76.4 0.1 copy.38
  76.5 0.0 copy-start.6
  76.6 1.1 subtract_convert_fusion
  77.7 0.1 maximum_bitcast_fusion
  77.8 0.9 slice_bitcast_fusion
  78.7 0.1 fusion.2
  78.8 0.1 compare_reduce_fusion
  78.9 0.6 slice_bitcast_fusion.1
  79.5 1.0 fusion.1
  80.5 0.6 slice_bitcast_fusion.3
  81.2 0.0 copy-done.6
  81.2 0.3 fusion
  81.5 0.1 maximum_maximum_fusion
  81.7 0.9 copy.31
  82.6 2.2 copy.32.q_ref
  84.7 18.7 %attention.1 = bf16[2,256,512]{2,1,0:T(8,128)(2,1)} custom-call(s32[64]{0:T(128)} %select_reduce_fusion.inv_ref, s32[1]{0:T(128)} %bitcast.1.blk_ref, bf16[2,640,256]{2,1,0:T(8,128)(2,1)} %copy.32.q_ref, bf16[64,128,640]{2,1,0:T(8,128)(2,1)} %bitcast.69), custom_call_target="tpu_custom_call" | custom-call | tf_op jit(solution)/shard_map/attention/pallas_call | solution.py:278
  103.4 0.0 copy-start.3
  103.4 1.2 copy.33
  104.7 0.0 copy-done.7
  104.7 0.3 convolution_convert_fusion.3
  105.0 0.1 copy-done.3
  105.2 0.5 convolution_convert_fusion
  105.7 14.0 %tp_scatter.1 = bf16[4,32,2048]{2,1,0:T(8,128)(2,1)S(1)} custom-call(bf16[4,32,2048]{2,1,0:T(8,128)(2,1)S(1)} %bitcast.68), custom_call_target="tpu_custom_call" | custom-call | tf_op jit(solution)/shard_map/tp_scatter/pallas_call | solution.py:447
  119.7 0.1 convert_reduce_fusion
  119.7 0.0 copy-done.4
  119.7 0.2 fusion.7
  119.9 0.0 copy-done.8
  119.9 0.1 fusion.9.p_ref
  120.0 17.3 %column_gather.1 = bf16[8,32,2048]{2,1,0:T(8,128)(2,1)S(1)} custom-call(bf16[32,2048]{1,0:T(8,128)(2,1)S(1)} %fusion.9.p_ref), custom_call_target="tpu_custom_call" | custom-call | tf_op jit(solution)/shard_map/column_gather/pallas_call | solution.py:359
  137.4 0.0 copy-start.2
  137.4 1.0 copy-done.2
  138.4 105.5 %experts.1 = bf16[256,2048]{1,0:T(8,128)(2,1)} custom-call(bf16[256,2048]{1,0:T(8,128)(2,1)} %bitcast.67, f32[4,8,256]{2,1,0:T(8,128)} %get-tuple-element.24.sla, f32[4,8,256]{2,1,0:T(8,128)} %get-tuple-element.23.slb, f32[4,8,256]{2,1,0:T(8,128)} %get-tuple-element.22.gta, f32[4,8,256]{2,1,0:T(8,128)} %get-tuple-element.21.gtb, bf16[352,2048]{1,0:T(8,128)(2,1)} %bitcast.74, ...), custom_call_target="tpu_custom_call" | custom-call | tf_op jit(solution)/shard_map/experts/pallas_call | solution.py:716
  243.9 0.0 copy-start.1
  243.9 1.2 copy-done.1
  245.1 15.6 %column_scatter.1 = f32[32,2048]{1,0:T(8,128)S(1)} custom-call(bf16[8,32,2048]{2,1,0:T(8,128)(2,1)S(1)} %bitcast.66), custom_call_target="tpu_custom_call" | custom-call | tf_op jit(solution)/shard_map/column_scatter/pallas_call | solution.py:427
  260.7 0.7 fusion.10
  (15 shorter events, 0.1 us)
Async XLA Ops:
  0.0 74.6 %copy-start = (bf16[2048,768]{1,0:T(8,128)(2,1)S(1)}, bf16[2048,768]{1,0:T(8,128)(2,1)}, u32[]{:S(2)}) copy-start(bf16[2048,768]{1,0:T(8,128)(2,1)} %param.18) | copy-start | bytes 9437188
  0.0 12.5 %copy-start.9 = (f32[512]{0:T(512)S(1)}, f32[512]{0:T(512)}, u32[]{:S(2)}) copy-start(f32[512]{0:T(512)} %param.20) | copy-start | bytes 6148
  9.7 4.5 %copy-start.5 = (bf16[32,2048]{1,0:T(8,128)(2,1)}, bf16[32,2048]{1,0:T(8,128)(2,1)S(1)}, u32[]{:S(2)}) copy-start(bf16[32,2048]{1,0:T(8,128)(2,1)S(1)} %fusion.5.nt_ref) | copy-start | bytes 393220
  76.5 4.6 %copy-start.6 = (bf16[4,512,128]{2,1,0:T(8,128)(2,1)S(1)}, bf16[4,512,128]{2,1,0:T(8,128)(2,1)}, u32[]{:S(2)}) copy-start(bf16[4,512,128]{2,1,0:T(8,128)(2,1)} %param.21) | copy-start | bytes 1572868
  84.7 19.9 %copy-start.7 = (bf16[4,512,128]{2,1,0:T(8,128)(2,1)S(1)}, bf16[4,512,128]{2,1,0:T(8,128)(2,1)}, u32[]{:S(2)}) copy-start(bf16[4,512,128]{2,1,0:T(8,128)(2,1)} %param.22) | copy-start | bytes 1572868
  103.4 1.8 copy-start.3
  105.2 14.6 %copy-start.4 = (bf16[32,2048]{1,0:T(8,128)(2,1)S(1)}, bf16[32,2048]{1,0:T(8,128)(2,1)}, u32[]{:S(2)}) copy-start(bf16[32,2048]{1,0:T(8,128)(2,1)} %param.15) | copy-start | bytes 393220
  105.2 14.7 %copy-start.8 = (f32[2048]{0:T(1024)S(1)}, f32[2048]{0:T(1024)}, u32[]{:S(2)}) copy-start(f32[2048]{0:T(1024)} %param.24) | copy-start | bytes 24580
  137.4 1.0 copy-start.2
  243.9 1.2 copy-start.1

commit v4 on v1

v4 whole, which is shorter than its diff:
```python
import functools
import math

import jax
import jax.numpy as jnp
from jax import lax
from jax.experimental import pallas as pl
from jax.experimental.pallas import tpu as pltpu
from jax.sharding import PartitionSpec as P

EPSILON = 1e-06
MESH = pl.DeviceIdType.MESH
BF = jnp.bfloat16
F32 = jnp.float32
KEYW = 640


def place():
    s = lax.axis_index("seq")
    t = lax.axis_index("tp")
    return (s // 32) * 4 + t, (s // 8) % 4, (s // 2) % 4, s % 2


def dev(z, y, x, c):
    z, y, x, c = z % 8, y % 4, x % 4, c % 2
    return ((z // 4) * 32 + y * 8 + x * 2 + c, z % 4)


def greet(peers):
    barrier = pltpu.get_barrier_semaphore()
    for p in peers:
        pl.semaphore_signal(barrier, inc=1, device_id=p, device_id_type=MESH)
    pl.semaphore_wait(barrier, len(peers))


def rcopy(src, dst, ss, rs, device):
    return pltpu.make_async_remote_copy(
        src_ref=src, dst_ref=dst, send_sem=ss, recv_sem=rs, device_id=device, device_id_type=MESH
    )


def normalize(values, gain_vec):
    values = values.astype(F32)
    factor = lax.rsqrt(jnp.mean(values * values, axis=-1, keepdims=True) + EPSILON)
    return values * factor * gain_vec


def rotate(values, position):
    half_width = values.shape[-1] // 2
    frequency = jnp.exp(
        jnp.arange(half_width, dtype=F32) * (-2.0 * math.log(10000.0) / values.shape[-1])
    )
    angles = position.astype(F32).reshape(position.shape + (1,) * (values.ndim - 1)) * frequency
    cosine = jnp.cos(angles)
    sine_part = jnp.sin(angles)
    first_half = values[..., :half_width]
    second_half = values[..., half_width:]
    return jnp.concatenate(
        [
            first_half * cosine - second_half * sine_part,
            second_half * cosine + first_half * sine_part,
        ],
        axis=-1,
    )


def gather_kernel(
    kv_ref, nt_ref, rg_ref, qw_ref, uk_ref, cos_ref, sin_ref, KV, QO, RG, NT, ssem, rsem, lsem
):
    z, y, x, c = place()
    zh, t = z // 4, z % 4
    peers = [dev(z + k, y, x, c) for k in range(1, 8)]
    xs = [dev(z, y, x + 1, c), dev(z, y, x + 3, c), dev(z, y, x + 2, c)]
    ys = [dev(z, y + 1, x, c), dev(z, y + 3, x, c), dev(z, y + 2, x, c)]
    other = dev(z, y, x, c + 1)
    greet(peers + xs + ys + [other])
    number = [0]
    sent = []

    def send(src, dst, device):
        i = number[0]
        number[0] += 1
        cp = rcopy(src, dst, ssem.at[i], rsem.at[i], device)
        cp.start()
        sent.append(cp)
        return i

    def arrived(i, region):
        rcopy(region, region, ssem.at[i], rsem.at[i], other).wait_recv()

    rows = pl.ds(pl.multiple_of(t * 32, 32), 32)
    zi = {}
    mine = KV.at[zh, y, x, c, rows]
    for k in (4, 3, 5, 2, 6, 1, 7):
        zi[k] = send(kv_ref, mine, dev(z + k, y, x, c))
    locals_ = [
        pltpu.make_async_copy(kv_ref, mine, lsem.at[0]),
        pltpu.make_async_copy(nt_ref, NT.at[t], lsem.at[1]),
        pltpu.make_async_copy(rg_ref, RG.at[0, 0, zh], lsem.at[2]),
    ]
    for cp in locals_:
        cp.start()
    ri = send(rg_ref, RG.at[0, 0, zh], dev(z + 4, y, x, c))
    ti = {}
    for k in (3, 2, 1):
        ti[k] = send(nt_ref, NT.at[t], (zh * 32 + y * 8 + x * 2 + c, (t + k) % 4))
    for cp in locals_:
        cp.wait()
    for k in zi:
        zz = (z - k + 8) % 8
        arrived(zi[k], KV.at[zz // 4, y, x, c, pl.ds(pl.multiple_of((zz % 4) * 32, 32), 32)])
    arrived(ri, RG.at[0, 0, 1 - zh])
    spare = pltpu.make_async_copy(RG.at[0, 0], RG.at[1, 0], lsem.at[2])
    spare.start()
    routes_sent = []
    for p, k in ((1, 1), (2, 3), (3, 2)):
        g = RG.at[0, 0]
        routes_sent.append((send(g, RG.at[0, p], dev(z, y, x + k, c)), RG.at[0, p]))
        routes_sent.append((send(g, RG.at[1, p], dev(z, y + k, x, c)), RG.at[1, p]))
    lo, hi = pl.ds(0, 64), pl.ds(64, 64)
    xm, xp, xo = (x + 3) % 4, (x + 1) % 4, (x + 2) % 4
    ym, yp, yo = (y + 3) % 4, (y + 1) % 4, (y + 2) % 4
    a, b = KV.at[0, y, x, c], KV.at[1, y, x, c]
    ap = send(a, a, xs[0])
    am = send(a, a, xs[1])
    bp = send(b, b, ys[0])
    bm = send(b, b, ys[1])
    arrived(ap, KV.at[0, y, xm, c])
    g = KV.at[0, y, xm, c, lo]
    ap2 = send(g, g, xs[0])
    arrived(bp, KV.at[1, ym, x, c])
    g = KV.at[1, ym, x, c, lo]
    bp2 = send(g, g, ys[0])
    arrived(am, KV.at[0, y, xp, c])
    g = KV.at[0, y, xp, c, hi]
    am2 = send(g, g, xs[1])
    arrived(bm, KV.at[1, yp, x, c])
    g = KV.at[1, yp, x, c, hi]
    bm2 = send(g, g, ys[1])
    arrived(ap2, KV.at[0, y, xo, c, lo])
    arrived(am2, KV.at[0, y, xo, c, hi])
    r = KV.at[0, y, :, c]
    rp = send(r, r, ys[0])
    rm = send(r, r, ys[1])
    arrived(bp2, KV.at[1, yo, x, c, lo])
    arrived(bm2, KV.at[1, yo, x, c, hi])
    q = KV.at[1, :, x, c]
    qp = send(q, q, xs[0])
    qm = send(q, q, xs[1])
    across = [send(r, r, other), send(q, q, other)]
    for k in ti:
        arrived(ti[k], NT.at[(t - k + 4) % 4])
    queries = jnp.dot(
        NT[...].reshape(128, 2048), qw_ref[...], preferred_element_type=F32
    ).T.astype(BF)
    lane = lax.broadcasted_iota(jnp.int32, (576, 128), 1)
    for pair in (0, 1):
        heads = []
        for h in (2 * pair, 2 * pair + 1):
            at = h * 192
            long = jnp.dot(uk_ref[h], queries[at : at + 128], preferred_element_type=F32)
            one = queries[at + 128 : at + 160].astype(F32)
            two = queries[at + 160 : at + 192].astype(F32)
            turned = [one * cos_ref[...] - two * sin_ref[...],
                      two * cos_ref[...] + one * sin_ref[...]]
            heads.append(jnp.concatenate([long] + turned, axis=0))
        cols = pl.ds(pair * 128, 128)
        QO[0, 0:576, cols] = jnp.where(lane < 64, heads[0], pltpu.roll(heads[1], 64, 1)).astype(BF)
        QO[1, 0:576, cols] = jnp.where(lane < 64, pltpu.roll(heads[0], 64, 1), heads[1]).astype(BF)
    QO[:, 576:640, :] = jnp.zeros((2, 64, 256), BF)
    arrived(rp, KV.at[0, ym, :, c])
    g = KV.at[0, ym, :, c, lo]
    rp2 = send(g, g, ys[0])
    arrived(qp, KV.at[1, :, xm, c])
    g = KV.at[1, :, xm, c, lo]
    qp2 = send(g, g, xs[0])
    arrived(rm, KV.at[0, yp, :, c])
    g = KV.at[0, yp, :, c, hi]
    rm2 = send(g, g, ys[1])
    arrived(qm, KV.at[1, :, xp, c])
    g = KV.at[1, :, xp, c, hi]
    qm2 = send(g, g, xs[1])
    for g in (KV.at[0, ym, :, c], KV.at[1, :, xm, c], KV.at[0, yp, :, c], KV.at[1, :, xp, c]):
        across.append(send(g, g, other))
    arrived(rp2, KV.at[0, yo, :, c, lo])
    arrived(rm2, KV.at[0, yo, :, c, hi])
    g = KV.at[0, yo, :, c]
    across.append(send(g, g, other))
    arrived(qp2, KV.at[1, :, xo, c, lo])
    arrived(qm2, KV.at[1, :, xo, c, hi])
    g = KV.at[1, :, xo, c]
    across.append(send(g, g, other))
    d = 1 - c
    for i, region in zip(
        across,
        (
            KV.at[0, y, :, d],
            KV.at[1, :, x, d],
            KV.at[0, ym, :, d],
            KV.at[1, :, xm, d],
            KV.at[0, yp, :, d],
            KV.at[1, :, xp, d],
            KV.at[0, yo, :, d],
            KV.at[1, :, xo, d],
        ),
    ):
        arrived(i, region)
    spare.wait()
    for i, region in routes_sent:
        arrived(i, region)
    for cp in sent:
        cp.wait_send()


def gather_keys(kv_own, normed_own, rg, qw, uk, cosine, sine):
    count = 48
    vm = pl.BlockSpec(memory_space=pltpu.VMEM)
    return pl.pallas_call(
        gather_kernel,
        out_shape=(
            jax.ShapeDtypeStruct((2, 4, 4, 2, 128, KEYW), BF),
            jax.ShapeDtypeStruct((2, KEYW, 256), BF),
            jax.ShapeDtypeStruct((2, 4, 2, 4, 16, 32), F32),
        ),
        in_specs=[vm] * 7,
        out_specs=(pl.BlockSpec(memory_space=pltpu.HBM), vm, vm),
        scratch_shapes=[
            pltpu.VMEM((4, 32, 2048), BF),
            pltpu.SemaphoreType.DMA((count,)),
            pltpu.SemaphoreType.DMA((count,)),
            pltpu.SemaphoreType.DMA((3,)),
        ],
        compiler_params=pltpu.CompilerParams(
            collective_id=0, has_side_effects=True, vmem_limit_bytes=60 * 2**20
        ),
        name="gather_keys",
    )(kv_own, normed_own, rg, qw, uk, cosine, sine)


CHUNK = 1024


def attention_kernel(inv_ref, blk_ref, q_ref, kv_hbm, o_ref, kbuf, m_ref, l_ref, acc_ref, sems):
    low = blk_ref[0]
    per = CHUNK // 64
    top_chunks = (127 - low) // per + 1

    def issue(p, carry):
        second = p >= 64
        d = inv_ref[jnp.where(second, 127 - p, p)]
        off = pl.multiple_of(jnp.where(second, 64, 0), 64)
        pltpu.make_async_copy(
            kv_hbm.at[d, pl.ds(off, 64)],
            kbuf.at[pl.ds(pl.multiple_of(p * 64, 64), 64)],
            sems.at[p // per],
        ).start()
        return carry

    lax.fori_loop(0, top_chunks * per, issue, 0)
    scale = (128 + 64) ** (-0.5)

    for half in (1, 0):
        block = low if half == 0 else 127 - low
        last = block // per
        m_ref[...] = jnp.full_like(m_ref, -1e30)
        l_ref[...] = jnp.zeros_like(l_ref)
        acc_ref[...] = jnp.zeros_like(acc_ref)

        def step(ch, masked):
            region = kbuf.at[pl.ds(pl.multiple_of(ch * CHUNK, CHUNK), CHUNK)]
            if half == 1:
                pltpu.make_async_copy(region, region, sems.at[ch]).wait()
            keys = region[...]
            s = jnp.dot(keys, q_ref[half], preferred_element_type=F32) * scale
            if masked:
                key = lax.broadcasted_iota(jnp.int32, s.shape, 0)
                query = lax.broadcasted_iota(jnp.int32, s.shape, 1) % 64
                s = jnp.where(key - query <= block * 64 - ch * CHUNK, s, -1e30)
            m_old = m_ref[...]
            m_new = jnp.maximum(m_old, jnp.max(s, axis=0, keepdims=True))
            p = jnp.exp(s - m_new)
            alpha = jnp.exp(m_old - m_new)
            l_ref[...] = l_ref[...] * alpha + jnp.sum(p, axis=0, keepdims=True)
            m_ref[...] = m_new
            acc_ref[...] = acc_ref[...] * alpha + lax.dot_general(
                keys[:, :512], p.astype(BF), (((0,), (0,)), ((), ())), preferred_element_type=F32
            )

        def loop(ch, carry):
            step(ch, False)
            return carry

        lax.fori_loop(0, last, loop, 0)
        step(last, True)
        o_ref[half] = (acc_ref[...] / l_ref[...]).T.astype(BF)


def attention(inv, low, q, kv):
    return pl.pallas_call(
        attention_kernel,
        out_shape=jax.ShapeDtypeStruct((2, 256, 512), BF),
        in_specs=[
            pl.BlockSpec(memory_space=pltpu.SMEM),
            pl.BlockSpec(memory_space=pltpu.SMEM),
            pl.BlockSpec(memory_space=pltpu.VMEM),
            pl.BlockSpec(memory_space=pltpu.HBM),
        ],
        out_specs=pl.BlockSpec(memory_space=pltpu.VMEM),
        scratch_shapes=[
            pltpu.VMEM((8192, KEYW), BF),
            pltpu.VMEM((1, 256), F32),
            pltpu.VMEM((1, 256), F32),
            pltpu.VMEM((512, 256), F32),
            pltpu.SemaphoreType.DMA((8192 // CHUNK,)),
        ],
        compiler_params=pltpu.CompilerParams(vmem_limit_bytes=60 * 2**20),
        name="attention",
    )(inv, low, q, kv)


def tp_scatter_kernel(p_ref, o_ref, ssem, rsem, lsem):
    z, y, x, c = place()
    s, t = lax.axis_index("seq"), lax.axis_index("tp")
    greet([(s, (t + k) % 4) for k in (1, 2, 3)])
    cps = []
    for k in (2, 3, 1):
        to = (t + k) % 4
        cp = rcopy(p_ref.at[to], o_ref.at[k], ssem.at[k], rsem.at[k], (s, to))
        cp.start()
        cps.append(cp)
    own = pltpu.make_async_copy(p_ref.at[t], o_ref.at[0], lsem)
    own.start()
    own.wait()
    for cp in cps:
        cp.wait()


def exchange(kernel, name, cid, array, out):
    vm = pl.BlockSpec(memory_space=pltpu.VMEM)
    return pl.pallas_call(
        kernel,
        out_shape=jax.ShapeDtypeStruct(out, BF),
        in_specs=[vm],
        out_specs=vm,
        scratch_shapes=[
            pltpu.SemaphoreType.DMA((8,)),
            pltpu.SemaphoreType.DMA((8,)),
            pltpu.SemaphoreType.DMA,
        ],
        compiler_params=pltpu.CompilerParams(
            collective_id=cid, has_side_effects=True, vmem_limit_bytes=16 * 2**20
        ),
        name=name,
    )(array)


def experts_kernel(
    own, slots, gates, wg, wu, wd, out,
    X, S, R, O, M, T, rbuf, sbuf, home, H, Qs, Q,
    sx, rx, sz, rz, s2, r2, s3, r3, sr, rr, s4, r4, sf, rf, sq, rq, lsem,
):
    z, y, x, c = place()
    towards = [dev(z + 1, y, x, c), dev(z + 7, y, x, c)]
    peers = towards + [dev(z, y, x, c + 1)]
    for k in (1, 2, 3):
        for d in (0, 1):
            peers.append(dev(z, y + k, x, c + d))
            peers.append(dev(z, y, x + k, c + d))
    greet(peers)
    odd = z % 2

    def first(p, k):
        return rcopy(
            own, X.at[z, p], sx.at[p], rx.at[p], dev(z, y + k * odd, x + k * (1 - odd), c)
        )

    def opposite(r):
        o = (z + r) % 2
        return dev(z, y + 2 * o, x + 2 * (1 - o), c)

    for p, k in ((1, 1), (2, 3)):
        first(p, k).start()
    here = pltpu.make_async_copy(own, X.at[z, 0], lsem)
    here.start()

    def shard(d, s):
        return (z + 8 - s) % 8 if d == 0 else (z + s) % 8

    def ring(d, s, h):
        part = X.at[shard(d, s - 1), pl.ds(0, 3), pl.ds(16 * h, 16)]
        return rcopy(part, part, sz.at[d, s - 1, h], rz.at[d, s - 1, h], towards[d])

    def fourth(r):
        u = (z + r) % 8
        return rcopy(X.at[u, 0], X.at[u, 3], sf.at[r], rf.at[r], opposite(r))

    here.wait()
    first(1, 1).wait_recv()
    first(2, 3).wait_recv()
    for h in (0, 1):
        for d in (0, 1):
            ring(d, 1, h).start()
    fourth(0).start()

    def rows16(j):
        return pl.ds(j * 16, 16)

    def partner(r, j, sign):
        o = (z + r) % 2
        step = (j // 2) * sign + 4
        return dev(z, y + step * (1 - o), x + step * o, c + j % 2)

    def hop2(r, j):
        return rcopy(
            S.at[r, rows16(j)], R.at[r, rows16(j)], s2.at[r, j], r2.at[r, j], partner(r, j, 1)
        )

    def hop3(r, j):
        return rcopy(
            O.at[r, rows16(j)], M.at[r, rows16(j)], s3.at[r, j], r3.at[r, j], partner(r, j, -1)
        )

    number = lax.broadcasted_iota(jnp.int32, (8, 16, 32), 1).astype(F32)

    def table(r, scale=None):
        u = (z + r) % 8
        parts = []
        for p in range(4):
            part = (slots[u, p][:, None, :] == number).astype(F32)
            if scale is not None:
                part = part * scale[u, p][:, None, :]
            parts.append(part.reshape(128, 32))
        return jnp.concatenate(parts, axis=1)

    def spread(r):
        tokens = X[(z + r) % 8].reshape(128, 2048)
        S[r] = jnp.dot(
            table(r).astype(BF), tokens, preferred_element_type=F32
        ).astype(BF)
        for j in (4, 5, 2, 6, 3, 7, 1):
            hop2(r, j).start()
        R[r, 0:16] = S[r, 0:16]

    def across(rows, weight):
        return lax.dot_general(
            rows, weight[...], (((1,), (1,)), ((), ())), preferred_element_type=F32
        )

    def work(ra, rb):
        for r in (ra, rb):
            for j in range(1, 8):
                hop2(r, j).wait_recv()
        rows = jnp.concatenate([R[ra], R[rb]], axis=0)
        gate = across(rows, wg)
        up = across(rows, wu)
        hidden = (gate / (1.0 + jnp.exp(-gate)) * up).astype(BF)
        result = jnp.dot(hidden, wd[...], preferred_element_type=F32).astype(BF)
        O[ra] = result[:128]
        O[rb] = result[128:]
        M[ra, 0:16] = result[0:16]
        M[rb, 0:16] = result[128:144]
        for r in (ra, rb):
            for j in (4, 5, 2, 6, 3, 7, 1):
                hop3(r, j).start()

    def pass_on(s, h):
        for d in (0, 1):

            @pl.when((s < 4) | ((s == 4) & (h == d)))
            def _():
                part = X.at[shard(d, s), pl.ds(0, 3), pl.ds(16 * h, 16)]
                rcopy(part, part, sz.at[d, s - 1, h], rz.at[d, s - 1, h], towards[d]).wait_recv()

            @pl.when((s < 3) | ((s == 3) & (h == d)))
            def _():
                ring(d, s + 1, h).start()

    def step(s, carry):
        @pl.when(s < 5)
        def _():
            pass_on(s, 0)

        @pl.when(s < 6)
        def _():
            fourth((9 - s) % 8).wait_recv()
            spread((9 - s) % 8)

        @pl.when((s > 1) & (s < 5))
        def _():
            fourth(s - 1).wait_recv()
            spread(s - 1)

        @pl.when(s < 5)
        def _():
            pass_on(s, 1)
            fourth((8 - s) % 8).start()

        @pl.when(s < 4)
        def _():
            fourth(s).start()

        @pl.when(s > 2)
        def _():
            work((11 - s) % 8, s - 2)

        return carry

    lax.fori_loop(1, 7, step, 0)

    def quarter(r):
        return rcopy(Qs.at[r], Q.at[r], sq.at[r], rq.at[r], opposite(r))

    def weigh(r):
        for j in range(1, 8):
            hop3(r, j).wait_recv()
        w = table(r, gates)
        hi = w.astype(BF)
        lo = (w - hi.astype(F32)).astype(BF)
        dims = (((0,), (0,)), ((), ()))
        sums = lax.dot_general(hi, M[r], dims, preferred_element_type=F32) + lax.dot_general(
            lo, M[r], dims, preferred_element_type=F32
        )
        Qs[r] = sums[96:].astype(BF)
        T[r] = sums[:96]
        quarter(r).start()

    def joined(r):
        quarter(r).wait_recv()
        T[r, 0:32] = T[r, 0:32] + Q[r].astype(F32)

    def half(h):
        return pl.ds(h * 48, 48)

    def reduce(d, s, h):
        return rcopy(
            sbuf.at[d, s - 1, half(h)], rbuf.at[d, s - 1, half(h)],
            sr.at[d, s - 1, h], rr.at[d, s - 1, h], towards[d],
        )

    weigh(4)
    weigh(5)
    weigh(3)
    joined(4)
    for d in (0, 1):
        sbuf[d, 0, half(d)] = T[4, half(d)].astype(BF)
    for d in (0, 1):
        reduce(d, 1, d).start()

    def fold(s, carry):
        joined(5 - s)
        joined(3 + s)
        for h in (0, 1):
            for d, r in ((0, 5 - s), (1, 3 + s)):

                @pl.when((s > 2) | (h == d))
                def _():
                    reduce(d, s - 1, h).wait_recv()
                    sbuf[d, s - 1, half(h)] = (
                        T[r, half(h)] + rbuf[d, s - 2, half(h)].astype(F32)
                    ).astype(BF)

                @pl.when((s == 2) & (h != d))
                def _():
                    sbuf[d, s - 1, half(h)] = T[r, half(h)].astype(BF)

            for d in (0, 1):
                reduce(d, s, h).start()
        weigh(4 - s)

        @pl.when(s < 4)
        def _():
            weigh(4 + s)

        return carry

    lax.fori_loop(2, 5, fold, 0)
    joined(0)
    for h in (0, 1):
        for d in (0, 1):
            reduce(d, 4, h).wait_recv()
    T[0] = T[0] + rbuf[0, 3].astype(F32) + rbuf[1, 3].astype(F32)
    home[...] = T[0].astype(BF)

    def last(p, k):
        return rcopy(
            home.at[pl.ds(p * 32, 32)], H.at[p], s4.at[p], r4.at[p],
            dev(z, y + (4 - k) * odd, x + (4 - k) * (1 - odd), c),
        )

    total = T[0, 0:32]
    for p, k in ((1, 1), (2, 3)):
        last(p, k).start()
    for p, k in ((1, 1), (2, 3)):
        last(p, k).wait_recv()
        total += H[p].astype(F32)
    out[...] = total

    for p, k in ((1, 1), (2, 3)):
        first(p, k).wait_send()
        last(p, k).wait_send()
    for d in (0, 1):
        for s in (1, 2, 3, 4):
            for h in (0, 1):
                if s < 4 or h == d:
                    ring(d, s, h).wait_send()
                if s > 1 or h == d:
                    reduce(d, s, h).wait_send()

    def drain(r, carry):
        fourth(r).wait_send()
        quarter(r).wait_send()
        for j in range(1, 8):
            hop2(r, j).wait_send()
            hop3(r, j).wait_send()
        return carry

    lax.fori_loop(0, 8, drain, 0)


def experts(own, slots, gates, wg, wu, wd):
    vm = pl.BlockSpec(memory_space=pltpu.VMEM)
    big = pltpu.VMEM((8, 128, 2048), BF)
    dma = pltpu.SemaphoreType.DMA
    return pl.pallas_call(
        experts_kernel,
        out_shape=jax.ShapeDtypeStruct((32, 2048), F32),
        in_specs=[vm] * 6,
        out_specs=vm,
        scratch_shapes=[
            pltpu.VMEM((8, 4, 32, 2048), BF), big, big, big, big,
            pltpu.VMEM((8, 96, 2048), F32),
            pltpu.VMEM((2, 4, 96, 2048), BF),
            pltpu.VMEM((2, 4, 96, 2048), BF),
            pltpu.VMEM((96, 2048), BF),
            pltpu.VMEM((3, 32, 2048), BF),
            pltpu.VMEM((8, 32, 2048), BF),
            pltpu.VMEM((8, 32, 2048), BF),
            dma((4,)), dma((4,)),
            dma((2, 4, 2)), dma((2, 4, 2)),
            dma((8, 8)), dma((8, 8)), dma((8, 8)), dma((8, 8)),
            dma((2, 4, 2)), dma((2, 4, 2)),
            dma((4,)), dma((4,)),
            dma((8,)), dma((8,)), dma((8,)), dma((8,)),
            dma,
        ],
        compiler_params=pltpu.CompilerParams(
            collective_id=4, has_side_effects=True, vmem_limit_bytes=60 * 2**20
        ),
        name="experts",
    )(own, slots, gates, wg, wu, wd)


def slot_tables(rgs, z, y, x, c):
    plane = lax.broadcasted_iota(jnp.int32, (4, 2, 4, 16, 32), 2)
    mine = jnp.where(plane % 2 == 0, rgs[0], rgs[1])
    mine = mine.transpose(1, 2, 0, 3, 4).reshape(8, 4, 16, 32)
    routes = mine[:, :, :6].astype(jnp.int32)
    gates = mine[:, :, 8:14]
    off = jnp.arange(8, dtype=jnp.int32) // 2
    core = (c + jnp.arange(8, dtype=jnp.int32) % 2) % 2
    base = (z // 4) * 32
    along_y = base + ((y + off) % 4) * 8 + x * 2 + core
    along_x = base + y * 8 + ((x + off) % 4) * 2 + core
    u = jnp.arange(8, dtype=jnp.int32)[:, None]
    expert = jnp.where(u % 2 == 0, along_y[None], along_x[None])
    hit = routes[:, :, None] == expert[:, None, :, None, None]
    member = jnp.any(hit, axis=3)
    gate = jnp.sum(jnp.where(hit, gates[:, :, None], 0.0), axis=3)
    ti = lax.broadcasted_iota(jnp.int32, (32, 32), 0)
    tj = lax.broadcasted_iota(jnp.int32, (32, 32), 1)
    before = (ti < tj).astype(BF)
    rank = jnp.dot(
        member.astype(BF).reshape(256, 32), before, preferred_element_type=F32
    ).reshape(8, 4, 8, 32)
    place_ = lax.broadcasted_iota(jnp.int32, (8, 4, 8, 32), 1)
    slot = jnp.where(member, (place_ * 4).astype(F32) + rank, -1.0)
    return slot, gate


def body(
    tokens, block_ids, attn_gain, q_weight, kv_weight, kv_gain, uk_weight, uv_weight,
    o_weight, ffn_gain, w_gate, w_up, w_down, routes, gate_weights,
):
    z, y, x, c = place()
    t = lax.axis_index("tp")
    s = lax.axis_index("seq")
    own_blocks = lax.dynamic_slice(block_ids, (s, 0), (1, 2))[0]
    normed_own = normalize(tokens, attn_gain).astype(BF)
    own_pos = own_blocks[t // 2] * 64 + (t % 2) * 32 + jnp.arange(32, dtype=jnp.int32)
    projected = jnp.dot(normed_own, kv_weight, preferred_element_type=F32)
    latent = normalize(projected[:, :512], kv_gain).astype(BF)
    key_rope = rotate(projected[:, 512:], own_pos).astype(BF)
    kv_own = jnp.concatenate([latent, key_rope, jnp.zeros((32, 64), BF)], axis=1)
    pad2 = jnp.zeros((4, 32, 2), F32)
    rg = jnp.concatenate(
        [
            routes.astype(F32).reshape(4, 32, 6), pad2,
            gate_weights.reshape(4, 32, 6), pad2,
        ],
        axis=2,
    ).transpose(0, 2, 1)
    query_pos = (own_blocks[:, None] * 64 + jnp.arange(64, dtype=jnp.int32)[None, :]).reshape(128)
    frequency = jnp.exp(jnp.arange(32, dtype=F32) * (-2.0 * math.log(10000.0) / 64))
    angles = frequency[:, None] * query_pos.astype(F32)[None, :]
    kv, q, rgs = gather_keys(
        kv_own, normed_own, rg, q_weight, uk_weight, jnp.cos(angles), jnp.sin(angles)
    )
    ids = jnp.arange(64, dtype=jnp.int32)
    inv = jnp.sum(
        jnp.where(block_ids[:, 0][None, :] == ids[:, None], ids[None, :], 0), axis=1
    ).astype(jnp.int32)
    out_latent = attention(inv, own_blocks[:1], q, kv.reshape(64, 128, KEYW))
    out_latent = out_latent.reshape(2, 4, 64, 512).transpose(1, 0, 2, 3).reshape(4, 128, 512)
    head_out = jnp.einsum(
        "htl,hlv->thv", out_latent, uv_weight, preferred_element_type=F32
    ).astype(BF)
    partial_out = jnp.dot(head_out.reshape(128, 512), o_weight, preferred_element_type=F32)
    parts = exchange(
        tp_scatter_kernel, "tp_scatter", 1, partial_out.astype(BF).reshape(4, 32, 2048),
        (4, 32, 2048),
    )
    attn_own = jnp.sum(parts.astype(F32), axis=0)
    mixed = (tokens.astype(F32) + attn_own).astype(BF)
    normed_ffn = normalize(mixed, ffn_gain).astype(BF)
    slots, gates = slot_tables(rgs, z, y, x, c)
    sums = experts(normed_ffn, slots, gates, w_gate[0].T, w_up[0].T, w_down[0])
    return (mixed.astype(F32) + sums).astype(BF)


def solution(mesh):
    return jax.shard_map(
        body,
        mesh=mesh,
        in_specs=(
            P(("seq", "tp"), None), P(), P(), P(None, "tp"), P(), P(),
            P("tp", None, None), P("tp", None, None), P("tp", None), P(),
            P("seq", None, "tp"), P("seq", None, "tp"), P("seq", "tp", None),
            P("seq", None), P("seq", None),
        ),
        out_specs=P(("seq", "tp"), None),
        check_vma=False,
    )
```

time: 318 us -> 253 us (0.80); the launches traced: 317 us -> 248 us
  Pallas kernels: 272 us -> 231 us
  local copies, waits for them, and re-layouts: 20.4 us -> 3.76 us
  matrix products: 16.4 us -> 2.4 us
    pallas_call x3 -> x1, Pallas kernels: 72.3 us -> 14.6 us  [exchange(): pl.pallas_call(kernel, out_shape=jax.ShapeDtypeStruct(out, BF), in_specs=...]
    unnamed x39 -> x20, local copies, waits for them, and re-layouts: 17.4 us -> 0.19 us
    pallas_call x1, Pallas kernels: 117 us -> 134 us  [experts(): pl.pallas_call(experts_kernel, out_shape=jax.ShapeDtypeStruct((32, 2048),...]
    dot_general x9 -> x1, matrix products: 13.2 us -> 0.8 us  [slot_tables(): jnp.dot(member.astype(BF).reshape(256, 32), before, preferred_element_typ...]
    pallas_call x1, Pallas kernels: 27.9 us -> 18.7 us  [attention(): pl.pallas_call(attention_kernel, out_shape=jax.ShapeDtypeStruct((2, 256,...]
    pallas_call x1, Pallas kernels: 54.8 us -> 64 us  [gather_keys(): pl.pallas_call(gather_kernel, out_shape=(jax.ShapeDtypeStruct((2, 4, 4, 2...]
where the time goes in v4:
time: 253 us; the launch traced here: 248 us
  Pallas kernels  231 us (91%)
  other arithmetic  10.3 us (4%)
  local copies, waits for them, and re-layouts  3.76 us (1%)
    pallas_call x1, Pallas kernels, experts(): pl.pallas_call(experts_kernel, out_shape=jax.ShapeDtypeStruct((32, 2048),...  134 us
    pallas_call x1, Pallas kernels, gather_keys(): pl.pallas_call(gather_kernel, out_shape=(jax.ShapeDtypeStruct((2, 4, 4, 2...  64 us
    pallas_call x1, Pallas kernels, attention(): pl.pallas_call(attention_kernel, out_shape=jax.ShapeDtypeStruct((2, 256,...  18.7 us
    pallas_call x1, Pallas kernels, exchange(): pl.pallas_call(kernel, out_shape=jax.ShapeDtypeStruct(out, BF), in_specs=...  14.6 us

profile of v4, /device:TPU:1, one launch (start us, length us, event | category | flops | bytes accessed | tf_op | source)
XLA Modules:
  0.0 248.3 jit_solution(15991602255366839836)
XLA Ops:
  0.0 0.0 copy-start
  0.0 0.0 copy-start.8
  0.0 0.0 copy-start.9
  0.0 0.0 copy-start.6
  0.0 0.0 copy-start.7
  0.2 0.1 broadcast_select_fusion
  0.2 1.4 dynamic_slice.7
  2.3 1.0 fusion.2
  3.3 1.0 fusion.4.nt_ref
  4.4 0.0 copy-done
  4.4 0.0 copy-start.3
  4.4 0.8 fusion.32
  5.2 0.1 fusion.15
  5.3 0.1 multiply_reduce_fusion
  5.5 0.0 copy-done.9
  5.5 0.1 multiply_convert_fusion
  5.6 0.1 pad.7.clone
  5.6 0.7 maximum_maximum_fusion.kv_ref
  6.3 0.0 copy-done.8
  6.3 0.2 multiply_reduce_fusion.1
  6.5 0.1 add_convert_fusion
  6.6 0.1 convert_element_type.71
  6.7 0.8 multiply_sine_fusion
  7.4 0.0 copy-done.6
  7.4 0.1 reshape.226
  7.5 0.0 copy-done.7
  7.5 0.1 reshape.227
  7.6 0.6 maximum_bitcast_fusion.rg_ref
  8.2 0.0 copy-done.3
  8.2 64.0 %gather_keys.1 = (bf16[2,4,4,2,128,640]{5,4,3,2,1,0:T(8,128)(2,1)}, bf16[2,640,256]{2,1,0:T(8,128)(2,1)}, f32[2,4,2,4,16,32]{5,4,3,2,1,0:T(8,128)}) custom-call(bf16[32,640]{1,0:T(8,128)(2,1)} %maximum_maximum_fusion.kv_ref, bf16[32,2048]{1,0:T(8,128)(2,1)} %copy-done.3, f32[4,16,32]{2,1,0:T(8,128)} %maximum_bitcast_fusion.rg_ref, bf16[2048,768]{1,0:T(8,128)(2,1)} %qw_ref.1, ...), custom_call_target="tpu_custom_call" | custom-call | tf_op jit(solution)/shard_map/gather_keys/pallas_call | solution.py:218
  72.2 1.1 bitcast_select_fusion
  73.5 0.8 fusion.1.gates
  74.3 0.2 compare_reduce_fusion
  74.5 0.8 fusion.slots
  75.3 0.6 slice.34
  75.9 0.6 select_reduce_fusion.inv_ref
  76.5 0.0 copy-start.4
  76.5 18.7 %attention.1 = bf16[2,256,512]{2,1,0:T(8,128)(2,1)} custom-call(s32[64]{0:T(128)} %select_reduce_fusion.inv_ref, s32[1]{0:T(128)} %bitcast.1.blk_ref, bf16[2,640,256]{2,1,0:T(8,128)(2,1)} %get-tuple-element.8.q_ref, bf16[64,128,640]{2,1,0:T(8,128)(2,1)} %bitcast.46), custom_call_target="tpu_custom_call" | custom-call | tf_op jit(solution)/shard_map/attention/pallas_call | solution.py:299
  95.2 0.0 copy-start.1
  95.2 1.2 copy.34
  96.5 0.0 copy-done.4
  96.5 0.3 convolution_convert_fusion.1
  96.8 0.1 copy-done.1
  97.0 0.0 copy-start.2
  97.0 0.0 copy-start.5
  97.0 0.5 convolution_convert_fusion
  97.4 14.6 %tp_scatter.1 = bf16[4,32,2048]{2,1,0:T(8,128)(2,1)S(1)} custom-call(bf16[4,32,2048]{2,1,0:T(8,128)(2,1)S(1)} %bitcast.45), custom_call_target="tpu_custom_call" | custom-call | tf_op jit(solution)/shard_map/tp_scatter/pallas_call | solution.py:340
  112.1 0.1 convert_reduce_fusion
  112.2 0.0 copy-done.2
  112.2 0.2 fusion.6
  112.3 0.0 copy-done.5
  112.3 0.8 fusion.8.own
  113.1 133.6 %experts.1 = f32[32,2048]{1,0:T(8,128)} custom-call(bf16[32,2048]{1,0:T(8,128)(2,1)} %fusion.8.own, f32[8,4,8,32]{3,2,1,0:T(8,128)} %fusion.slots, f32[8,4,8,32]{3,2,1,0:T(8,128)} %fusion.1.gates, bf16[352,2048]{1,0:T(8,128)(2,1)} %bitcast.49, bf16[352,2048]{1,0:T(8,128)(2,1)} %bitcast.50, bf16[352,2048]{1,0:T(8,128)(2,1)} %bitcast.51), custom_call_target="tpu_custom_call" | custom-call | tf_op jit(solution)/shard_map/experts/pallas_call | solution.py:624
  246.7 1.6 fusion.9
  (19 shorter events, 0.2 us)
Async XLA Ops:
  0.0 4.4 %copy-start = (bf16[2048,576]{0,1:T(8,128)(2,1)S(1)}, bf16[2048,576]{0,1:T(8,128)(2,1)}, u32[]{:S(2)}) copy-start(bf16[2048,576]{0,1:T(8,128)(2,1)} %param.19) | copy-start | bytes 7077892
  0.0 6.3 %copy-start.8 = (s32[64,2]{0,1:T(2,128)S(1)}, s32[64,2]{0,1:T(2,128)}, u32[]{:S(2)}) copy-start(s32[64,2]{0,1:T(2,128)} %param.16) | copy-start | bytes 1540
  0.0 5.5 %copy-start.9 = (f32[512]{0:T(512)S(1)}, f32[512]{0:T(512)}, u32[]{:S(2)}) copy-start(f32[512]{0:T(512)} %param.20) | copy-start | bytes 6148
  0.0 7.4 %copy-start.6 = (s32[128,6]{0,1:T(8,128)S(1)}, s32[128,6]{0,1:T(8,128)}, u32[]{:S(2)}) copy-start(s32[128,6]{0,1:T(8,128)} %param.28) | copy-start | bytes 9220
  0.0 7.5 %copy-start.7 = (f32[128,6]{0,1:T(8,128)S(1)}, f32[128,6]{0,1:T(8,128)}, u32[]{:S(2)}) copy-start(f32[128,6]{0,1:T(8,128)} %param.29) | copy-start | bytes 9220
  4.4 3.9 %copy-start.3 = (bf16[32,2048]{1,0:T(8,128)(2,1)}, bf16[32,2048]{1,0:T(8,128)(2,1)S(1)}, u32[]{:S(2)}) copy-start(bf16[32,2048]{1,0:T(8,128)(2,1)S(1)} %fusion.4.nt_ref) | copy-start | bytes 393220
  76.5 20.0 %copy-start.4 = (bf16[4,512,128]{2,1,0:T(8,128)(2,1)S(1)}, bf16[4,512,128]{2,1,0:T(8,128)(2,1)}, u32[]{:S(2)}) copy-start(bf16[4,512,128]{2,1,0:T(8,128)(2,1)} %param.22) | copy-start | bytes 1572868
  95.2 1.8 copy-start.1
  97.0 15.2 %copy-start.2 = (bf16[32,2048]{1,0:T(8,128)(2,1)S(1)}, bf16[32,2048]{1,0:T(8,128)(2,1)}, u32[]{:S(2)}) copy-start(bf16[32,2048]{1,0:T(8,128)(2,1)} %param.15) | copy-start | bytes 393220
  97.0 15.4 %copy-start.5 = (f32[2048]{0:T(1024)S(1)}, f32[2048]{0:T(1024)}, u32[]{:S(2)}) copy-start(f32[2048]{0:T(1024)} %param.24) | copy-start | bytes 24580

commit v5 on v4

--- a/solution.py
+++ b/solution.py
@@ -459,53 +459,9 @@
         O[rb] = result[128:]
         M[ra, 0:16] = result[0:16]
         M[rb, 0:16] = result[128:144]
-        for r in (ra, rb):
+        for r in (rb, ra):
             for j in (4, 5, 2, 6, 3, 7, 1):
                 hop3(r, j).start()
-
-    def pass_on(s, h):
-        for d in (0, 1):
-
-            @pl.when((s < 4) | ((s == 4) & (h == d)))
-            def _():
-                part = X.at[shard(d, s), pl.ds(0, 3), pl.ds(16 * h, 16)]
-                rcopy(part, part, sz.at[d, s - 1, h], rz.at[d, s - 1, h], towards[d]).wait_recv()
-
-            @pl.when((s < 3) | ((s == 3) & (h == d)))
-            def _():
-                ring(d, s + 1, h).start()
-
-    def step(s, carry):
-        @pl.when(s < 5)
-        def _():
-            pass_on(s, 0)
-
-        @pl.when(s < 6)
-        def _():
-            fourth((9 - s) % 8).wait_recv()
-            spread((9 - s) % 8)
-
-        @pl.when((s > 1) & (s < 5))
-        def _():
-            fourth(s - 1).wait_recv()
-            spread(s - 1)
-
-        @pl.when(s < 5)
-        def _():
-            pass_on(s, 1)
-            fourth((8 - s) % 8).start()
-
-        @pl.when(s < 4)
-        def _():
-            fourth(s).start()
-
-        @pl.when(s > 2)
-        def _():
-            work((11 - s) % 8, s - 2)
-
-        return carry
-
-    lax.fori_loop(1, 7, step, 0)
 
     def quarter(r):
         return rcopy(Qs.at[r], Q.at[r], sq.at[r], rq.at[r], opposite(r))
@@ -524,6 +480,61 @@
         T[r] = sums[:96]
         quarter(r).start()
 
+    def weigh_pairs(first_one, last_one):
+        def one(i, carry):
+            weigh(jnp.where(i % 2 == 0, (8 - i // 2) % 8, i // 2 + 1))
+            return carry
+
+        lax.fori_loop(first_one, last_one, one, 0)
+
+    def pass_on(s, h):
+        for d in (0, 1):
+
+            @pl.when((s < 4) | ((s == 4) & (h == d)))
+            def _():
+                part = X.at[shard(d, s), pl.ds(0, 3), pl.ds(16 * h, 16)]
+                rcopy(part, part, sz.at[d, s - 1, h], rz.at[d, s - 1, h], towards[d]).wait_recv()
+
+            @pl.when((s < 3) | ((s == 3) & (h == d)))
+            def _():
+                ring(d, s + 1, h).start()
+
+    def step(s, carry):
+        @pl.when(s < 5)
+        def _():
+            pass_on(s, 0)
+
+        @pl.when(s < 6)
+        def _():
+            fourth((9 - s) % 8).wait_recv()
+            spread((9 - s) % 8)
+
+        @pl.when((s > 1) & (s < 5))
+        def _():
+            fourth(s - 1).wait_recv()
+            spread(s - 1)
+
+        @pl.when(s < 5)
+        def _():
+            pass_on(s, 1)
+            fourth((8 - s) % 8).start()
+
+        @pl.when(s < 4)
+        def _():
+            fourth(s).start()
+
+        @pl.when(s > 2)
+        def _():
+            work((11 - s) % 8, s - 2)
+
+        @pl.when(s > 4)
+        def _():
+            weigh_pairs(2 * s - 10, 2 * s - 8)
+
+        return carry
+
+    lax.fori_loop(1, 7, step, 0)
+
     def joined(r):
         quarter(r).wait_recv()
         T[r, 0:32] = T[r, 0:32] + Q[r].astype(F32)
@@ -537,9 +548,9 @@
             sr.at[d, s - 1, h], rr.at[d, s - 1, h], towards[d],
         )
 
+    weigh_pairs(4, 6)
     weigh(4)
     weigh(5)
-    weigh(3)
     joined(4)
     for d in (0, 1):
         sbuf[d, 0, half(d)] = T[4, half(d)].astype(BF)
@@ -565,12 +576,6 @@
 
             for d in (0, 1):
                 reduce(d, s, h).start()
-        weigh(4 - s)
-
-        @pl.when(s < 4)
-        def _():
-            weigh(4 + s)
-
         return carry
 
     lax.fori_loop(2, 5, fold, 0)

time: 253 us -> 258 us (1.020); the launches traced: 248 us -> 257 us
  Pallas kernels: 231 us -> 240 us
    pallas_call x1, Pallas kernels: 134 us -> 143 us  [experts(): pl.pallas_call(experts_kernel, out_shape=jax.ShapeDtypeStruct((32, 2048),...]
where the time goes in v5:
time: 258 us; the launch traced here: 257 us
  Pallas kernels  240 us (93%)
  other arithmetic  10.3 us (4%)
  local copies, waits for them, and re-layouts  3.76 us (1%)
    pallas_call x1, Pallas kernels, experts(): pl.pallas_call(experts_kernel, out_shape=jax.ShapeDtypeStruct((32, 2048),...  143 us
    pallas_call x1, Pallas kernels, gather_keys(): pl.pallas_call(gather_kernel, out_shape=(jax.ShapeDtypeStruct((2, 4, 4, 2...  64 us
    pallas_call x1, Pallas kernels, attention(): pl.pallas_call(attention_kernel, out_shape=jax.ShapeDtypeStruct((2, 256,...  18.5 us
    pallas_call x1, Pallas kernels, exchange(): pl.pallas_call(kernel, out_shape=jax.ShapeDtypeStruct(out, BF), in_specs=...  14.9 us

profile of v5, /device:TPU:1, one launch (start us, length us, event | category | flops | bytes accessed | tf_op | source)
XLA Modules:
  0.0 257.4 jit_solution(636304892118387220)
XLA Ops:
  0.0 0.0 copy-start
  0.0 0.0 copy-start.8
  0.0 0.0 copy-start.9
  0.0 0.0 copy-start.6
  0.0 0.0 copy-start.7
  0.2 0.1 broadcast_select_fusion
  0.2 1.4 dynamic_slice.7
  2.3 1.0 fusion.2
  3.3 1.0 fusion.4.nt_ref
  4.4 0.0 copy-done
  4.4 0.0 copy-start.3
  4.4 0.8 fusion.32
  5.2 0.1 fusion.15
  5.3 0.1 multiply_reduce_fusion
  5.5 0.0 copy-done.9
  5.5 0.1 multiply_convert_fusion
  5.6 0.1 pad.7.clone
  5.6 0.7 maximum_maximum_fusion.kv_ref
  6.3 0.0 copy-done.8
  6.3 0.2 multiply_reduce_fusion.1
  6.5 0.1 add_convert_fusion
  6.6 0.1 convert_element_type.71
  6.7 0.8 multiply_sine_fusion
  7.4 0.0 copy-done.6
  7.4 0.1 reshape.226
  7.5 0.0 copy-done.7
  7.5 0.1 reshape.227
  7.6 0.6 maximum_bitcast_fusion.rg_ref
  8.2 0.0 copy-done.3
  8.2 64.0 %gather_keys.1 = (bf16[2,4,4,2,128,640]{5,4,3,2,1,0:T(8,128)(2,1)}, bf16[2,640,256]{2,1,0:T(8,128)(2,1)}, f32[2,4,2,4,16,32]{5,4,3,2,1,0:T(8,128)}) custom-call(bf16[32,640]{1,0:T(8,128)(2,1)} %maximum_maximum_fusion.kv_ref, bf16[32,2048]{1,0:T(8,128)(2,1)} %copy-done.3, f32[4,16,32]{2,1,0:T(8,128)} %maximum_bitcast_fusion.rg_ref, bf16[2048,768]{1,0:T(8,128)(2,1)} %qw_ref.1, ...), custom_call_target="tpu_custom_call" | custom-call | tf_op jit(solution)/shard_map/gather_keys/pallas_call | solution.py:218
  72.2 1.1 bitcast_select_fusion
  73.5 0.8 fusion.1.gates
  74.3 0.2 compare_reduce_fusion
  74.5 0.8 fusion.slots
  75.3 0.6 slice.34
  75.9 0.6 select_reduce_fusion.inv_ref
  76.5 0.0 copy-start.4
  76.5 18.5 %attention.1 = bf16[2,256,512]{2,1,0:T(8,128)(2,1)} custom-call(s32[64]{0:T(128)} %select_reduce_fusion.inv_ref, s32[1]{0:T(128)} %bitcast.1.blk_ref, bf16[2,640,256]{2,1,0:T(8,128)(2,1)} %get-tuple-element.8.q_ref, bf16[64,128,640]{2,1,0:T(8,128)(2,1)} %bitcast.46), custom_call_target="tpu_custom_call" | custom-call | tf_op jit(solution)/shard_map/attention/pallas_call | solution.py:299
  95.0 0.0 copy-start.1
  95.1 1.2 copy.34
  96.3 0.0 copy-done.4
  96.3 0.4 convolution_convert_fusion.1
  96.7 0.1 copy-done.1
  96.8 0.0 copy-start.2
  96.8 0.0 copy-start.5
  96.8 0.5 convolution_convert_fusion
  97.3 14.9 %tp_scatter.1 = bf16[4,32,2048]{2,1,0:T(8,128)(2,1)S(1)} custom-call(bf16[4,32,2048]{2,1,0:T(8,128)(2,1)S(1)} %bitcast.45), custom_call_target="tpu_custom_call" | custom-call | tf_op jit(solution)/shard_map/tp_scatter/pallas_call | solution.py:340
  112.1 0.1 convert_reduce_fusion
  112.2 0.0 copy-done.2
  112.2 0.2 fusion.6
  112.4 0.0 copy-done.5
  112.4 0.8 fusion.8.own
  113.2 142.6 %experts.1 = f32[32,2048]{1,0:T(8,128)} custom-call(bf16[32,2048]{1,0:T(8,128)(2,1)} %fusion.8.own, f32[8,4,8,32]{3,2,1,0:T(8,128)} %fusion.slots, f32[8,4,8,32]{3,2,1,0:T(8,128)} %fusion.1.gates, bf16[352,2048]{1,0:T(8,128)(2,1)} %bitcast.49, bf16[352,2048]{1,0:T(8,128)(2,1)} %bitcast.50, bf16[352,2048]{1,0:T(8,128)(2,1)} %bitcast.51), custom_call_target="tpu_custom_call" | custom-call | tf_op jit(solution)/shard_map/experts/pallas_call | solution.py:629
  255.8 1.6 fusion.9
  (19 shorter events, 0.2 us)
Async XLA Ops:
  0.0 4.4 %copy-start = (bf16[2048,576]{0,1:T(8,128)(2,1)S(1)}, bf16[2048,576]{0,1:T(8,128)(2,1)}, u32[]{:S(2)}) copy-start(bf16[2048,576]{0,1:T(8,128)(2,1)} %param.19) | copy-start | bytes 7077892
  0.0 6.3 %copy-start.8 = (s32[64,2]{0,1:T(2,128)S(1)}, s32[64,2]{0,1:T(2,128)}, u32[]{:S(2)}) copy-start(s32[64,2]{0,1:T(2,128)} %param.16) | copy-start | bytes 1540
  0.0 5.5 %copy-start.9 = (f32[512]{0:T(512)S(1)}, f32[512]{0:T(512)}, u32[]{:S(2)}) copy-start(f32[512]{0:T(512)} %param.20) | copy-start | bytes 6148
  0.0 7.4 %copy-start.6 = (s32[128,6]{0,1:T(8,128)S(1)}, s32[128,6]{0,1:T(8,128)}, u32[]{:S(2)}) copy-start(s32[128,6]{0,1:T(8,128)} %param.28) | copy-start | bytes 9220
  0.0 7.5 %copy-start.7 = (f32[128,6]{0,1:T(8,128)S(1)}, f32[128,6]{0,1:T(8,128)}, u32[]{:S(2)}) copy-start(f32[128,6]{0,1:T(8,128)} %param.29) | copy-start | bytes 9220
  4.4 3.9 %copy-start.3 = (bf16[32,2048]{1,0:T(8,128)(2,1)}, bf16[32,2048]{1,0:T(8,128)(2,1)S(1)}, u32[]{:S(2)}) copy-start(bf16[32,2048]{1,0:T(8,128)(2,1)S(1)} %fusion.4.nt_ref) | copy-start | bytes 393220
  76.5 19.8 %copy-start.4 = (bf16[4,512,128]{2,1,0:T(8,128)(2,1)S(1)}, bf16[4,512,128]{2,1,0:T(8,128)(2,1)}, u32[]{:S(2)}) copy-start(bf16[4,512,128]{2,1,0:T(8,128)(2,1)} %param.22) | copy-start | bytes 1572868
  95.0 1.8 copy-start.1
  96.8 15.4 %copy-start.2 = (bf16[32,2048]{1,0:T(8,128)(2,1)S(1)}, bf16[32,2048]{1,0:T(8,128)(2,1)}, u32[]{:S(2)}) copy-start(bf16[32,2048]{1,0:T(8,128)(2,1)} %param.15) | copy-start | bytes 393220
  96.8 15.6 %copy-start.5 = (f32[2048]{0:T(1024)S(1)}, f32[2048]{0:T(1024)}, u32[]{:S(2)}) copy-start(f32[2048]{0:T(1024)} %param.24) | copy-start | bytes 24580

commit v6 on v4

--- a/solution.py
+++ b/solution.py
@@ -459,7 +459,7 @@
         O[rb] = result[128:]
         M[ra, 0:16] = result[0:16]
         M[rb, 0:16] = result[128:144]
-        for r in (ra, rb):
+        for r in (rb, ra):
             for j in (4, 5, 2, 6, 3, 7, 1):
                 hop3(r, j).start()
 
@@ -539,12 +539,12 @@
 
     weigh(4)
     weigh(5)
-    weigh(3)
     joined(4)
     for d in (0, 1):
         sbuf[d, 0, half(d)] = T[4, half(d)].astype(BF)
     for d in (0, 1):
         reduce(d, 1, d).start()
+    weigh(3)
 
     def fold(s, carry):
         joined(5 - s)

time: 253 us -> 253 us (level)
  no operation moved by 1% of the time
where the time goes in v6:
time: 253 us; the launch traced here: 249 us
  Pallas kernels  232 us (92%)
  other arithmetic  10.3 us (4%)
  local copies, waits for them, and re-layouts  3.76 us (1%)
    pallas_call x1, Pallas kernels, experts(): pl.pallas_call(experts_kernel, out_shape=jax.ShapeDtypeStruct((32, 2048),...  134 us
    pallas_call x1, Pallas kernels, gather_keys(): pl.pallas_call(gather_kernel, out_shape=(jax.ShapeDtypeStruct((2, 4, 4, 2...  64 us
    pallas_call x1, Pallas kernels, attention(): pl.pallas_call(attention_kernel, out_shape=jax.ShapeDtypeStruct((2, 256,...  18.7 us
    pallas_call x1, Pallas kernels, exchange(): pl.pallas_call(kernel, out_shape=jax.ShapeDtypeStruct(out, BF), in_specs=...  14.6 us

profile of v6, /device:TPU:1, one launch (start us, length us, event | category | flops | bytes accessed | tf_op | source)
XLA Modules:
  0.0 249.2 jit_solution(10574408460604938163)
XLA Ops:
  0.0 0.0 copy-start
  0.0 0.0 copy-start.8
  0.0 0.0 copy-start.9
  0.0 0.0 copy-start.6
  0.0 0.0 copy-start.7
  0.2 0.1 broadcast_select_fusion
  0.2 1.4 dynamic_slice.7
  2.3 1.0 fusion.2
  3.3 1.0 fusion.4.nt_ref
  4.4 0.0 copy-done
  4.4 0.0 copy-start.3
  4.4 0.8 fusion.32
  5.2 0.1 fusion.15
  5.3 0.1 multiply_reduce_fusion
  5.5 0.0 copy-done.9
  5.5 0.1 multiply_convert_fusion
  5.6 0.1 pad.7.clone
  5.6 0.7 maximum_maximum_fusion.kv_ref
  6.3 0.0 copy-done.8
  6.3 0.2 multiply_reduce_fusion.1
  6.5 0.1 add_convert_fusion
  6.6 0.1 convert_element_type.71
  6.7 0.8 multiply_sine_fusion
  7.4 0.0 copy-done.6
  7.4 0.1 reshape.226
  7.5 0.0 copy-done.7
  7.5 0.1 reshape.227
  7.6 0.6 maximum_bitcast_fusion.rg_ref
  8.2 0.0 copy-done.3
  8.2 64.0 %gather_keys.1 = (bf16[2,4,4,2,128,640]{5,4,3,2,1,0:T(8,128)(2,1)}, bf16[2,640,256]{2,1,0:T(8,128)(2,1)}, f32[2,4,2,4,16,32]{5,4,3,2,1,0:T(8,128)}) custom-call(bf16[32,640]{1,0:T(8,128)(2,1)} %maximum_maximum_fusion.kv_ref, bf16[32,2048]{1,0:T(8,128)(2,1)} %copy-done.3, f32[4,16,32]{2,1,0:T(8,128)} %maximum_bitcast_fusion.rg_ref, bf16[2048,768]{1,0:T(8,128)(2,1)} %qw_ref.1, ...), custom_call_target="tpu_custom_call" | custom-call | tf_op jit(solution)/shard_map/gather_keys/pallas_call | solution.py:218
  72.2 1.1 bitcast_select_fusion
  73.5 0.8 fusion.1.gates
  74.3 0.2 compare_reduce_fusion
  74.5 0.8 fusion.slots
  75.3 0.6 slice.34
  75.9 0.6 select_reduce_fusion.inv_ref
  76.5 0.0 copy-start.4
  76.5 18.7 %attention.1 = bf16[2,256,512]{2,1,0:T(8,128)(2,1)} custom-call(s32[64]{0:T(128)} %select_reduce_fusion.inv_ref, s32[1]{0:T(128)} %bitcast.1.blk_ref, bf16[2,640,256]{2,1,0:T(8,128)(2,1)} %get-tuple-element.8.q_ref, bf16[64,128,640]{2,1,0:T(8,128)(2,1)} %bitcast.46), custom_call_target="tpu_custom_call" | custom-call | tf_op jit(solution)/shard_map/attention/pallas_call | solution.py:299
  95.2 0.0 copy-start.1
  95.2 1.2 copy.34
  96.5 0.0 copy-done.4
  96.5 0.3 convolution_convert_fusion.1
  96.8 0.1 copy-done.1
  97.0 0.0 copy-start.2
  97.0 0.0 copy-start.5
  97.0 0.5 convolution_convert_fusion
  97.4 14.6 %tp_scatter.1 = bf16[4,32,2048]{2,1,0:T(8,128)(2,1)S(1)} custom-call(bf16[4,32,2048]{2,1,0:T(8,128)(2,1)S(1)} %bitcast.45), custom_call_target="tpu_custom_call" | custom-call | tf_op jit(solution)/shard_map/tp_scatter/pallas_call | solution.py:340
  112.1 0.1 convert_reduce_fusion
  112.2 0.0 copy-done.2
  112.2 0.2 fusion.6
  112.3 0.0 copy-done.5
  112.3 0.8 fusion.8.own
  113.1 134.5 %experts.1 = f32[32,2048]{1,0:T(8,128)} custom-call(bf16[32,2048]{1,0:T(8,128)(2,1)} %fusion.8.own, f32[8,4,8,32]{3,2,1,0:T(8,128)} %fusion.slots, f32[8,4,8,32]{3,2,1,0:T(8,128)} %fusion.1.gates, bf16[352,2048]{1,0:T(8,128)(2,1)} %bitcast.49, bf16[352,2048]{1,0:T(8,128)(2,1)} %bitcast.50, bf16[352,2048]{1,0:T(8,128)(2,1)} %bitcast.51), custom_call_target="tpu_custom_call" | custom-call | tf_op jit(solution)/shard_map/experts/pallas_call | solution.py:624
  247.6 1.6 fusion.9
  (19 shorter events, 0.2 us)
Async XLA Ops:
  0.0 4.4 %copy-start = (bf16[2048,576]{0,1:T(8,128)(2,1)S(1)}, bf16[2048,576]{0,1:T(8,128)(2,1)}, u32[]{:S(2)}) copy-start(bf16[2048,576]{0,1:T(8,128)(2,1)} %param.19) | copy-start | bytes 7077892
  0.0 6.3 %copy-start.8 = (s32[64,2]{0,1:T(2,128)S(1)}, s32[64,2]{0,1:T(2,128)}, u32[]{:S(2)}) copy-start(s32[64,2]{0,1:T(2,128)} %param.16) | copy-start | bytes 1540
  0.0 5.5 %copy-start.9 = (f32[512]{0:T(512)S(1)}, f32[512]{0:T(512)}, u32[]{:S(2)}) copy-start(f32[512]{0:T(512)} %param.20) | copy-start | bytes 6148
  0.0 7.4 %copy-start.6 = (s32[128,6]{0,1:T(8,128)S(1)}, s32[128,6]{0,1:T(8,128)}, u32[]{:S(2)}) copy-start(s32[128,6]{0,1:T(8,128)} %param.28) | copy-start | bytes 9220
  0.0 7.5 %copy-start.7 = (f32[128,6]{0,1:T(8,128)S(1)}, f32[128,6]{0,1:T(8,128)}, u32[]{:S(2)}) copy-start(f32[128,6]{0,1:T(8,128)} %param.29) | copy-start | bytes 9220
  4.4 3.9 %copy-start.3 = (bf16[32,2048]{1,0:T(8,128)(2,1)}, bf16[32,2048]{1,0:T(8,128)(2,1)S(1)}, u32[]{:S(2)}) copy-start(bf16[32,2048]{1,0:T(8,128)(2,1)S(1)} %fusion.4.nt_ref) | copy-start | bytes 393220
  76.5 20.0 %copy-start.4 = (bf16[4,512,128]{2,1,0:T(8,128)(2,1)S(1)}, bf16[4,512,128]{2,1,0:T(8,128)(2,1)}, u32[]{:S(2)}) copy-start(bf16[4,512,128]{2,1,0:T(8,128)(2,1)} %param.22) | copy-start | bytes 1572868
  95.2 1.8 copy-start.1
  97.0 15.2 %copy-start.2 = (bf16[32,2048]{1,0:T(8,128)(2,1)S(1)}, bf16[32,2048]{1,0:T(8,128)(2,1)}, u32[]{:S(2)}) copy-start(bf16[32,2048]{1,0:T(8,128)(2,1)} %param.15) | copy-start | bytes 393220
  97.0 15.4 %copy-start.5 = (f32[2048]{0:T(1024)S(1)}, f32[2048]{0:T(1024)}, u32[]{:S(2)}) copy-start(f32[2048]{0:T(1024)} %param.24) | copy-start | bytes 24580
